TPU v7x, 128 devices: a whole 4x4x4 slice. The times are simulated.
128 devices in a mesh: grp: 4 (over y), row: 32 (over z, x, core).
Axes of the slice: x: 4, y: 4, z: 4, core: 2. Of those that a mesh axis runs over, the one named last changes fastest.
Arguments:
- feats: bfloat16 [65536, 512], P(('grp', 'row')), may hold values from -6 to 6
- tile_vals: bfloat16 [12288, 128, 128], P(('grp', 'row')), may hold values from -0.1875 to 0.1875
- tile_rows: int32 [12288], P(('grp', 'row')), may hold values from 0 to 15, as said below
- tile_slots: int32 [12288], P(('grp', 'row')), may hold values from 0 to 31, as said below
- tile_count: int32 [128], P(('grp', 'row')), may hold values from 32 to 96, as said below
- send_list: int32 [128, 32, 1], P(('grp', 'row')), may hold values from 0 to 3
- w_in: bfloat16 [2, 512, 1024], replicated, may hold values from -0.25 to 0.25
- w_out: bfloat16 [2, 1024, 512], replicated, may hold values from -0.1875 to 0.1875
- cotangent: bfloat16 [65536, 512], P(('grp', 'row')), may hold values from -6 to 6
Outputs:
- feat_grad: bfloat16 [65536, 512], P(('grp', 'row'))
- w_in_grad: float32 [2, 512, 1024], P(None, ('grp', 'row'))
- w_out_grad: float32 [2, 1024, 512], P(None, ('grp', 'row'))
Inputs may be any that keep to these rules, and one draw needn't show every extreme that they name: send_list[d, r, c] is the own block (0 to 3) that device d sends as its c-th to the device at row index r of its grp. p = tile_rows[d * 96 + t] names block p % 4 of the device at grp index p // 4 and d's row index; each of the 16 values stands among the first 16 tiles of every device. `tile_slots`: slot s is the block that the device at row index s of the same grp sends to this device; each of the 32 slots stands among the first 32 tiles of every device. Only the first tile_count[d] tiles of device d are used; at least one device uses all 96.
All inputs are finite; a program needn't handle non-finite values.
Results may differ from a plain program's by a relative error of at most 0.017.
Values may be sent and summed in bfloat16 or wider, within the bound.
No kernel may reach another device: no remote copies, remote signals or barrier semaphores. Data moves between devices by JAX's collectives and lax.ppermute only.
A program may use at most 128 MiB of HBM per device.

v0:
```python
import functools

import jax
import jax.numpy as jnp
from jax import lax
from jax.experimental import pallas as pl
from jax.experimental.pallas import tpu as pltpu
from jax.sharding import Mesh
from jax.sharding import PartitionSpec as P

ROW = ("row_0", "row_1", "row_2")
GRP_ROW = ("grp", "row_0", "row_1", "row_2")
FAR = ("grp", "row_0", "row_1")
NEAR = "row_2"

eps = 1e-06
UNROLL = 4
CHUNKS = 2


def exchange(value, axis):
    return lax.all_to_all(value, axis, split_axis=0, concat_axis=0, tiled=True)


def pair_table(keys, key_count, sources, count):
    tile_cap = keys.shape[0]
    steps = -(-((tile_cap + key_count) // 2) // UNROLL) * UNROLL
    ids = jnp.arange(tile_cap, dtype=jnp.int32)
    key_ids = jnp.arange(key_count, dtype=jnp.int32)
    live = ids < count
    held = (keys[:, None] == key_ids[None, :]) & live[:, None]
    per_key = jnp.sum(held.astype(jnp.int32), axis=0)
    per_key_steps = (per_key + 1) // 2
    start = jnp.sum(jnp.where(key_ids[None, :] < key_ids[:, None], per_key_steps[None, :], 0), axis=1)
    before = (keys[:, None] == keys[None, :]) & (ids[None, :] < ids[:, None])
    rank = jnp.sum(before.astype(jnp.int32), axis=1)
    place = 2 * jnp.sum(jnp.where(held, start[None, :], 0), axis=1) + rank
    spots = jnp.arange(2 * steps, dtype=jnp.int32)
    hit = (place[None, :] == spots[:, None]) & live[None, :]
    tile_at = jnp.min(jnp.where(hit, ids[None, :], tile_cap), axis=1)
    source_at = jnp.max(jnp.where(hit, sources[None, :], 0), axis=1)
    step_ids = jnp.arange(steps, dtype=jnp.int32)
    total = jnp.sum(per_key_steps)
    target = jnp.sum((start[None, :] <= step_ids[:, None]).astype(jnp.int32), axis=1) - 1
    target = jnp.where(step_ids < total, target, key_count)
    first = jnp.max((start[None, :] == step_ids[:, None]).astype(jnp.int32), axis=1)
    first = jnp.where(step_ids < total, first, 1)
    turns = (total + UNROLL - 1) // UNROLL
    return jnp.concatenate([tile_at, source_at, target, first, turns[None]]), steps


def tiles_kernel(table, *refs, steps, transposed, piece_count, out_pieces):
    data_pieces = refs[:piece_count]
    tiles = refs[piece_count]
    outs = refs[piece_count + 1 : piece_count + 1 + out_pieces]
    data, tile_buf, acc, data_sems, tile_sem = refs[piece_count + 1 + out_pieces :]
    tile_cap, tile_len, _ = tiles.shape
    piece_len = data_pieces[0].shape[0]
    out_len = outs[0].shape[0]
    copies = [
        pltpu.make_async_copy(
            data_pieces[i], data.at[pl.ds(i * piece_len, piece_len)], data_sems.at[i]
        )
        for i in range(piece_count)
    ]
    copies.append(pltpu.make_async_copy(tiles, tile_buf.at[pl.ds(0, tile_cap)], tile_sem))
    for copy in copies:
        copy.start()
    tile_buf[tile_cap] = jnp.zeros((tile_len, tile_len), tile_buf.dtype)
    for copy in copies:
        copy.wait()

    def turn(index, carry):
        products = []
        for u in range(UNROLL):
            step = index * UNROLL + u
            tile_0 = tile_buf[table[2 * step]]
            tile_1 = tile_buf[table[2 * step + 1]]
            data_0 = data[table[2 * steps + 2 * step]]
            data_1 = data[table[2 * steps + 2 * step + 1]]
            values = jnp.concatenate([data_0, data_1], axis=0)
            if transposed:
                pair = jnp.concatenate([tile_0, tile_1], axis=0)
                dims = (((0,), (0,)), ((), ()))
            else:
                pair = jnp.concatenate([tile_0, tile_1], axis=1)
                dims = (((1,), (0,)), ((), ()))
            products.append(
                lax.dot_general(pair, values, dims, preferred_element_type=jnp.float32)
            )
        for u in range(UNROLL):
            step = index * UNROLL + u
            target = table[4 * steps + step]
            first = table[5 * steps + step]
            acc[target] = jnp.where(first == 1, 0.0, acc[target]) + products[u]
        return carry

    lax.fori_loop(0, table[6 * steps], turn, 0)

    for piece in range(out_pieces):

        def finish(index, carry, piece=piece):
            outs[piece][index] = acc[piece * out_len + index].astype(outs[piece].dtype)
            return carry

        lax.fori_loop(0, out_len, finish, 0, unroll=2)


def run_tiles(table, steps, pieces, tiles, out_count, out_pieces, transposed):
    tile_cap, tile_len, _ = tiles.shape
    piece_len, _, width = pieces[0].shape
    out_len = out_count // out_pieces
    return pl.pallas_call(
        functools.partial(
            tiles_kernel,
            steps=steps,
            transposed=transposed,
            piece_count=len(pieces),
            out_pieces=out_pieces,
        ),
        out_shape=[jax.ShapeDtypeStruct((out_len, tile_len, width), jnp.bfloat16)] * out_pieces,
        in_specs=[pl.BlockSpec(memory_space=pltpu.SMEM)]
        + [pl.BlockSpec(memory_space=pl.ANY)] * (len(pieces) + 1),
        out_specs=[pl.BlockSpec(memory_space=pltpu.VMEM)] * out_pieces,
        scratch_shapes=[
            pltpu.VMEM((piece_len * len(pieces), tile_len, width), jnp.bfloat16),
            pltpu.VMEM((tile_cap + 1, tile_len, tile_len), tiles.dtype),
            pltpu.VMEM((out_count + 1, tile_len, width), jnp.float32),
            pltpu.SemaphoreType.DMA((len(pieces),)),
            pltpu.SemaphoreType.DMA,
        ],
        name="tiles_t" if transposed else "tiles",
    )(table, *pieces, tiles)


def pick_kernel(choice, own, out, sems):
    def copy(slot):
        return pltpu.make_async_copy(own.at[choice[slot]], out.at[slot], sems.at[slot])

    def start(slot, carry):
        copy(slot).start()
        return carry

    def wait(slot, carry):
        copy(slot).wait()
        return carry

    lax.fori_loop(0, out.shape[0], start, 0)
    lax.fori_loop(0, out.shape[0], wait, 0)


def pick_blocks(choice, own, chunk, width):
    count = choice.shape[0]
    blocks, tile_len, _ = own.shape
    return pl.pallas_call(
        pick_kernel,
        grid=(1,),
        out_shape=jax.ShapeDtypeStruct((count, tile_len, width), own.dtype),
        in_specs=[
            pl.BlockSpec(memory_space=pltpu.SMEM),
            pl.BlockSpec((blocks, tile_len, width), lambda i: (0, 0, chunk)),
        ],
        out_specs=pl.BlockSpec(memory_space=pl.ANY),
        scratch_shapes=[pltpu.SemaphoreType.DMA((count,))],
        name="pick",
    )(choice, own)


def place_kernel(choice, returned, base, extra, out, acc):
    acc[...] = base[...].astype(jnp.float32) + extra[...]

    def add(index, carry):
        block = choice[index]
        acc[block] += returned[index].astype(jnp.float32)
        return carry

    lax.fori_loop(0, returned.shape[0], add, 0, unroll=4)
    out[...] = acc[...].astype(out.dtype)


def place_blocks(choice, returned, base, extra, chunk):
    count, tile_len, width = returned.shape
    block = (base.shape[0], tile_len, width)
    return pl.pallas_call(
        place_kernel,
        grid=(1,),
        out_shape=jax.ShapeDtypeStruct(block, base.dtype),
        in_specs=[
            pl.BlockSpec(memory_space=pltpu.SMEM),
            pl.BlockSpec((count, tile_len, width), lambda i: (0, 0, 0)),
            pl.BlockSpec(block, lambda i: (0, 0, chunk)),
            pl.BlockSpec(block, lambda i: (0, 0, chunk)),
        ],
        out_specs=pl.BlockSpec(block, lambda i: (0, 0, 0)),
        scratch_shapes=[pltpu.VMEM(block, jnp.float32)],
        name="place",
    )(choice, returned, base, extra)


def shifted(value, axis, step):
    length = lax.axis_size(axis)
    return lax.ppermute(value, axis, [(i, (i + step) % length) for i in range(length)])


def scatter_sum(value, axis):
    length = lax.axis_size(axis)
    position = lax.axis_index(axis)
    rows = value.shape[0] // length
    total = lax.dynamic_slice_in_dim(value, position * rows, rows, 0)
    for step in range(1, length):
        start = (position + step) % length * rows
        piece = lax.dynamic_slice_in_dim(value, start, rows, 0).astype(jnp.bfloat16)
        total = total + shifted(piece, axis, step).astype(jnp.float32)
    return total


def column_order(columns, parts):
    far = columns // 2 // parts // 4
    place = jnp.arange(columns, dtype=jnp.int32)
    half = place // (columns // 2)
    part = place % (columns // 2) // (far * 4)
    rest = place % (far * 4)
    device = rest // 4 * 2 + (lax.axis_index(NEAR) + half) % 2
    source = (device * parts + part) * 4 + rest % 4
    ids = jnp.arange(columns, dtype=jnp.int32)
    return (ids[:, None] == source[None, :]).astype(jnp.bfloat16)


def reduce_weights(units, d_pre, activated, grad, unit_order, act_order, after):
    contract_rows = (((0,), (0,)), ((), ()))
    ordered_units = jnp.dot(units, unit_order).reshape(units.shape[0], 2, 1, -1)
    ordered_acts = jnp.dot(activated, act_order).reshape(units.shape[0], 2, 2, -1)
    halves = []
    for half in range(2):
        terms = [
            lax.dot_general(left, right, contract_rows, preferred_element_type=jnp.float32)
            for left, right in (
                (ordered_units[:, half, 0], d_pre),
                (ordered_acts[:, half, 0], grad),
                (ordered_acts[:, half, 1], grad),
            )
        ]
        halves.append(jnp.concatenate([term.astype(jnp.bfloat16) for term in terms], axis=1))
    halves[1], _ = lax.optimization_barrier((halves[1], after))
    total = halves[0].astype(jnp.float32) + shifted(halves[1], NEAR, 1).astype(jnp.float32)
    return scatter_sum(total, FAR[0])


def body(feats, tile_vals, tile_rows, tile_slots, tile_count, send_list, w_in, w_out, cotangent):
    row_count = lax.axis_size(ROW)
    grp_count = lax.axis_size("grp")
    node_count, width = feats.shape
    tile_len = tile_vals.shape[1]
    per_dev = node_count // tile_len
    slot_count = row_count
    panel_len = grp_count * per_dev
    layer_count = w_in.shape[0]
    count = tile_count[0]
    outgoing = send_list[0].reshape(slot_count)
    chunk_width = width // CHUNKS
    grp_id = lax.axis_index("grp")
    near_rows = (tile_rows // per_dev - grp_id) % grp_count * per_dev + tile_rows % per_dev
    row_table, row_steps = pair_table(near_rows, panel_len, tile_slots, count)
    slot_table, slot_steps = pair_table(tile_slots, slot_count, near_rows, count)
    factor = float(node_count * lax.axis_size(GRP_ROW)) ** (-0.5)
    unit_order = column_order(width, 1)
    act_order = column_order(w_in.shape[2], 2)
    contract_cols = (((1,), (1,)), ((), ()))
    hidden = feats
    saved = []
    for layer in range(layer_count):
        own_blocks = hidden.reshape(per_dev, tile_len, width)
        messages = []
        for chunk in range(CHUNKS):
            slot_data = exchange(pick_blocks(outgoing, own_blocks, chunk, chunk_width), ROW)
            pieces = run_tiles(
                row_table, row_steps, [slot_data], tile_vals, panel_len, grp_count, False
            )
            total = pieces[0].astype(jnp.float32)
            for step in (2, 1, 3):
                total = total + shifted(pieces[step], "grp", step).astype(jnp.float32)
            messages.append(total.reshape(node_count, chunk_width))
        message = jnp.concatenate(messages, axis=1)
        summed = message + hidden.astype(jnp.float32)
        norm_scale = lax.rsqrt(jnp.mean(summed * summed, axis=-1, keepdims=True) + eps)
        normed = summed * norm_scale
        normed_b = normed.astype(jnp.bfloat16)
        pre_act = jnp.dot(normed_b, w_in[layer], preferred_element_type=jnp.float32)
        activated = jax.nn.silu(pre_act).astype(jnp.bfloat16)
        update = jnp.dot(activated, w_out[layer], preferred_element_type=jnp.float32)
        saved.append((norm_scale, normed, normed_b, pre_act, activated))
        hidden = (hidden.astype(jnp.float32) + update).astype(jnp.bfloat16)
    grad_now = cotangent
    sums = [None] * layer_count
    for layer in reversed(range(layer_count)):
        norm_scale, normed, normed_b, pre_act, activated = saved[layer]
        d_act = lax.dot_general(
            grad_now, w_out[layer], contract_cols, preferred_element_type=jnp.float32
        )
        sigma = jax.nn.sigmoid(pre_act)
        d_pre = (d_act * sigma * (1.0 + pre_act * (1.0 - sigma))).astype(jnp.bfloat16)
        d_unit = lax.dot_general(
            d_pre, w_in[layer], contract_cols, preferred_element_type=jnp.float32
        )
        d_summed = norm_scale * (
            d_unit - normed * jnp.mean(d_unit * normed, axis=-1, keepdims=True)
        )
        d_summed_b, *late = lax.optimization_barrier(
            (d_summed.astype(jnp.bfloat16), normed_b, d_pre, activated, grad_now)
        )
        block_dims = (per_dev, tile_len, width)
        grad_blocks = grad_now.reshape(block_dims)
        d_blocks = d_summed.reshape(block_dims)
        d_blocks_b = d_summed_b.reshape(block_dims)
        updated = []
        for chunk in range(CHUNKS):
            own = d_blocks_b[:, :, chunk * chunk_width : (chunk + 1) * chunk_width]
            if chunk:
                own, _ = lax.optimization_barrier((own, per_slot))
            pieces = [own] + [shifted(own, "grp", grp_count - step) for step in range(1, grp_count)]
            per_slot = run_tiles(slot_table, slot_steps, pieces, tile_vals, slot_count, 1, True)[0]
            if chunk == (CHUNKS - 1 if layer else 0):
                sums[layer] = reduce_weights(
                    *late, unit_order, act_order, per_slot
                )
            returned = exchange(per_slot, ROW)
            updated.append(place_blocks(outgoing, returned, grad_blocks, d_blocks, chunk))
        grad_now = jnp.concatenate(updated, axis=2).reshape(node_count, width)
        if layer:
            grad_now, sums[layer] = lax.optimization_barrier((grad_now, sums[layer]))
    total = jnp.concatenate(sums, axis=1)
    for axis in FAR[1:]:
        total = scatter_sum(total, axis)
    total = total.reshape(total.shape[0], layer_count, -1) * factor
    split = w_in.shape[2]
    w_in_grad = jnp.swapaxes(total[:, :, :split], 0, 1)
    out_parts = total[:, :, split:].reshape(-1, layer_count, 2, width)
    w_out_grad = out_parts.transpose(1, 2, 0, 3).reshape(layer_count, -1, width)
    return (grad_now, w_in_grad, w_out_grad)


def solution(mesh):
    torus = Mesh(
        mesh.devices.reshape(mesh.shape["grp"], 4, 4, 2), ("grp", "row_0", "row_1", "row_2")
    )
    in_specs = (
        P(GRP_ROW, None),
        P(GRP_ROW, None, None),
        P(GRP_ROW),
        P(GRP_ROW),
        P(GRP_ROW),
        P(GRP_ROW, None, None),
        P(),
        P(),
        P(GRP_ROW, None),
    )
    out_specs = (P(GRP_ROW, None), P(None, GRP_ROW, None), P(None, GRP_ROW, None))
    return jax.shard_map(body, mesh=torus, in_specs=in_specs, out_specs=out_specs, check_vma=False)
```

profile of v0, /device:TPU:32, one launch (start us, length us, event | category | flops | bytes accessed | tf_op | source)
XLA Modules:
  0.0 428.5 jit_solution(18239840655008466052)
XLA Ops:
  3.2 8.1 %all-to-all-start.1 = ((bf16[32,128,256]{2,1,0:T(8,128)(2,1)}), bf16[32,128,256]{2,1,0:T(8,128)(2,1)S(1)}, u32[]{:S(2)}, u32[]{:S(2)}) async-start(bf16[32,128,256]{2,1,0:T(8,128)(2,1)} %pick.5), calls=%async_computation.1 | async-start | bytes 4194304 | tf_op jit(solution)/shard_map/all_to_all | solution.py:22
  15.7 22.2 %all-to-all-done.1.refs_0_ = bf16[32,128,256]{2,1,0:T(8,128)(2,1)S(1)} async-done(((bf16[32,128,256]{2,1,0:T(8,128)(2,1)}), bf16[32,128,256]{2,1,0:T(8,128)(2,1)S(1)}, u32[]{:S(2)}, u32[]{:S(2)}) %all-to-all-start.1) | async-done | bytes 2097184 | tf_op jit(solution)/shard_map/all_to_all | solution.py:22
  39.2 8.1 %all-to-all-start = ((bf16[32,128,256]{2,1,0:T(8,128)(2,1)}), bf16[32,128,256]{2,1,0:T(8,128)(2,1)}, u32[]{:S(2)}, u32[]{:S(2)}) async-start(bf16[32,128,256]{2,1,0:T(8,128)(2,1)} %pick.4), calls=%async_computation | async-start | bytes 4194304 | tf_op jit(solution)/shard_map/all_to_all | solution.py:22
  51.4 6.1 %tiles.5 = (bf16[4,128,256]{2,1,0:T(8,128)(2,1)}, bf16[4,128,256]{2,1,0:T(8,128)(2,1)}, bf16[4,128,256]{2,1,0:T(8,128)(2,1)}, bf16[4,128,256]{2,1,0:T(8,128)(2,1)}) custom-call(s32[337]{0:T(512)} %concatenate.34.table, bf16[32,128,256]{2,1,0:T(8,128)(2,1)} %copy-done.2, bf16[96,128,128]{2,1,0:T(8,128)(2,1)} %refs_4_.7), custom_call_target="tpu_custom_call" | custom-call | tf_op jit(solution)/shard_map/tiles/pallas_call | solution.py:113
  57.5 5.0 %collective-permute-start.3 = (bf16[4,128,256]{2,1,0:T(8,128)(2,1)}, bf16[4,128,256]{2,1,0:T(8,128)(2,1)S(1)}, u32[]{:S(2)}, u32[]{:S(2)}) collective-permute-start(bf16[4,128,256]{2,1,0:T(8,128)(2,1)} %get-tuple-element.40), channel_id=1, source_target_pairs={{0,64},{32,96},{64,0},{96,32},{1,65},{33,97},{65,1},{97,33},{2,66}... | collective-permute-start | bytes 786440 | tf_op jit(solution)/shard_map/ppermute | solution.py:202
  62.5 3.2 collective-permute-start.5
  65.8 8.2 %all-to-all-done.refs_0_ = bf16[32,128,256]{2,1,0:T(8,128)(2,1)} async-done(((bf16[32,128,256]{2,1,0:T(8,128)(2,1)}), bf16[32,128,256]{2,1,0:T(8,128)(2,1)}, u32[]{:S(2)}, u32[]{:S(2)}) %all-to-all-start) | async-done | bytes 2097184 | tf_op jit(solution)/shard_map/all_to_all | solution.py:22
  74.0 6.1 %tiles.4 = (bf16[4,128,256]{2,1,0:T(8,128)(2,1)}, bf16[4,128,256]{2,1,0:T(8,128)(2,1)}, bf16[4,128,256]{2,1,0:T(8,128)(2,1)}, bf16[4,128,256]{2,1,0:T(8,128)(2,1)}) custom-call(s32[337]{0:T(512)} %concatenate.34.table, bf16[32,128,256]{2,1,0:T(8,128)(2,1)} %all-to-all-done.refs_0_, bf16[96,128,128]{2,1,0:T(8,128)(2,1)} %refs_4_.7), custom_call_target="tpu_custom_call" | custom-call | tf_op jit(solution)/shard_map/tiles/pallas_call | solution.py:113
  80.1 5.0 %collective-permute-start = (bf16[4,128,256]{2,1,0:T(8,128)(2,1)}, bf16[4,128,256]{2,1,0:T(8,128)(2,1)S(1)}, u32[]{:S(2)}, u32[]{:S(2)}) collective-permute-start(bf16[4,128,256]{2,1,0:T(8,128)(2,1)} %get-tuple-element.36), channel_id=1, source_target_pairs={{0,64},{32,96},{64,0},{96,32},{1,65},{33,97},{65,1},{97,33},{2,66}... | collective-permute-start | bytes 786440 | tf_op jit(solution)/shard_map/ppermute | solution.py:202
  85.2 3.2 collective-permute-start.2
  88.6 4.0 collective-permute-done
  92.6 3.9 collective-permute-done.1
  105.9 6.2 %all-to-all-start.3 = ((bf16[32,128,256]{2,1,0:T(8,128)(2,1)}), bf16[32,128,256]{2,1,0:T(8,128)(2,1)}, u32[]{:S(2)}, u32[]{:S(2)}) async-start(bf16[32,128,256]{2,1,0:T(8,128)(2,1)} %pick.7), calls=%async_computation.3 | async-start | bytes 4194304 | tf_op jit(solution)/shard_map/all_to_all | solution.py:22
  114.8 23.7 %all-to-all-done.3.refs_0_ = bf16[32,128,256]{2,1,0:T(8,128)(2,1)} async-done(((bf16[32,128,256]{2,1,0:T(8,128)(2,1)}), bf16[32,128,256]{2,1,0:T(8,128)(2,1)}, u32[]{:S(2)}, u32[]{:S(2)}) %all-to-all-start.3) | async-done | bytes 2097184 | tf_op jit(solution)/shard_map/all_to_all | solution.py:22
  138.5 8.4 %all-to-all-start.2 = ((bf16[32,128,256]{2,1,0:T(8,128)(2,1)}), bf16[32,128,256]{2,1,0:T(8,128)(2,1)}, u32[]{:S(2)}, u32[]{:S(2)}) async-start(bf16[32,128,256]{2,1,0:T(8,128)(2,1)} %pick.6), calls=%async_computation.2 | async-start | bytes 4194304 | tf_op jit(solution)/shard_map/all_to_all | solution.py:22
  147.6 6.2 %tiles.7 = (bf16[4,128,256]{2,1,0:T(8,128)(2,1)}, bf16[4,128,256]{2,1,0:T(8,128)(2,1)}, bf16[4,128,256]{2,1,0:T(8,128)(2,1)}, bf16[4,128,256]{2,1,0:T(8,128)(2,1)}) custom-call(s32[337]{0:T(512)} %concatenate.34.table, bf16[32,128,256]{2,1,0:T(8,128)(2,1)} %all-to-all-done.3.refs_0_, bf16[96,128,128]{2,1,0:T(8,128)(2,1)} %refs_4_.7), custom_call_target="tpu_custom_call" | custom-call | tf_op jit(solution)/shard_map/tiles/pallas_call | solution.py:113
  153.8 4.0 collective-permute-start.9
  157.9 3.2 collective-permute-start.11
  162.6 11.0 %all-to-all-done.2.refs_0_ = bf16[32,128,256]{2,1,0:T(8,128)(2,1)} async-done(((bf16[32,128,256]{2,1,0:T(8,128)(2,1)}), bf16[32,128,256]{2,1,0:T(8,128)(2,1)}, u32[]{:S(2)}, u32[]{:S(2)}) %all-to-all-start.2) | async-done | bytes 2097184 | tf_op jit(solution)/shard_map/all_to_all | solution.py:22
  173.6 6.2 %tiles.6 = (bf16[4,128,256]{2,1,0:T(8,128)(2,1)}, bf16[4,128,256]{2,1,0:T(8,128)(2,1)}, bf16[4,128,256]{2,1,0:T(8,128)(2,1)}, bf16[4,128,256]{2,1,0:T(8,128)(2,1)}) custom-call(s32[337]{0:T(512)} %concatenate.34.table, bf16[32,128,256]{2,1,0:T(8,128)(2,1)} %all-to-all-done.2.refs_0_, bf16[96,128,128]{2,1,0:T(8,128)(2,1)} %refs_4_.7), custom_call_target="tpu_custom_call" | custom-call | tf_op jit(solution)/shard_map/tiles/pallas_call | solution.py:113
  179.7 4.0 collective-permute-start.6
  183.8 3.4 collective-permute-start.8
  187.3 3.9 collective-permute-done.6
  191.2 4.6 %collective-permute-done.7 = bf16[4,128,256]{2,1,0:T(8,128)(2,1)S(1)} collective-permute-done((bf16[4,128,256]{2,1,0:T(8,128)(2,1)}, bf16[4,128,256]{2,1,0:T(8,128)(2,1)S(1)}, u32[]{:S(2)}, u32[]{:S(2)}) %collective-permute-start.7) | collective-permute-done | bytes 262176 | tf_op jit(solution)/shard_map/ppermute | solution.py:202
  205.8 2.7 collective-permute-start.13
  214.5 6.2 %collective-permute-done.13.refs_2_ = bf16[4,128,256]{2,1,0:T(8,128)(2,1)} collective-permute-done((bf16[4,128,256]{2,1,0:T(8,128)(2,1)}, bf16[4,128,256]{2,1,0:T(8,128)(2,1)}, u32[]{:S(2)}, u32[]{:S(2)}) %collective-permute-start.13) | collective-permute-done | bytes 262176 | tf_op jit(solution)/shard_map/ppermute | solution.py:202
  220.7 6.9 %tiles_t.4 = bf16[32,128,256]{2,1,0:T(8,128)(2,1)} custom-call(s32[385]{0:T(512)} %concatenate.33.table, bf16[4,128,256]{2,1,0:T(8,128)(2,1)} %get-tuple-element.102.refs_0_, bf16[4,128,256]{2,1,0:T(8,128)(2,1)} %collective-permute-done.12.refs_1_, bf16[4,128,256]{2,1,0:T(8,128)(2,1)} %collective-permute-done.13.refs_2_, ...), custom_call_target="tpu_custom_call" | custom-call | tf_op jit(solution)/shard_map/tiles_t/pallas_call | solution.py:113
  227.6 7.3 %all-to-all-start.4 = ((bf16[32,128,256]{2,1,0:T(8,128)(2,1)}), bf16[32,128,256]{2,1,0:T(8,128)(2,1)}, u32[]{:S(2)}, u32[]{:S(2)}) async-start(bf16[32,128,256]{2,1,0:T(8,128)(2,1)} %tiles_t.4), calls=%async_computation.4 | async-start | bytes 4194304 | tf_op jit(solution)/shard_map/all_to_all | solution.py:22
  239.3 2.6 collective-permute-start.16
  244.0 10.1 %collective-permute-done.17.refs_3_ = bf16[4,128,256]{2,1,0:T(8,128)(2,1)S(1)} collective-permute-done((bf16[4,128,256]{2,1,0:T(8,128)(2,1)S(1)}, bf16[4,128,256]{2,1,0:T(8,128)(2,1)S(1)}, u32[]{:S(2)}, u32[]{:S(2)}) %collective-permute-start.17) | collective-permute-done | bytes 262176 | tf_op jit(solution)/shard_map/ppermute | solution.py:202
  255.5 7.0 %tiles_t.5 = bf16[32,128,256]{2,1,0:T(8,128)(2,1)} custom-call(s32[385]{0:T(512)} %concatenate.33.table, bf16[4,128,256]{2,1,0:T(8,128)(2,1)} %copy-done.13, bf16[4,128,256]{2,1,0:T(8,128)(2,1)} %collective-permute-done.15.refs_1_, bf16[4,128,256]{2,1,0:T(8,128)(2,1)} %copy-done.27, bf16[4,128,256]{2,1,0:T(8,128)(2,1)} %copy-done.26, ...), custom_call_target="tpu_custom_call" | custom-call | tf_op jit(solution)/shard_map/tiles_t/pallas_call | solution.py:113
  264.0 8.0 %all-to-all-start.5 = ((bf16[32,128,256]{2,1,0:T(8,128)(2,1)}), bf16[32,128,256]{2,1,0:T(8,128)(2,1)}, u32[]{:S(2)}, u32[]{:S(2)}) async-start(bf16[32,128,256]{2,1,0:T(8,128)(2,1)} %tiles_t.5), calls=%async_computation.5 | async-start | bytes 4194304 | tf_op jit(solution)/shard_map/all_to_all | solution.py:22
  281.1 7.2 %collective-permute-done.19 = bf16[64,2048]{1,0:T(8,128)(2,1)S(1)} collective-permute-done((bf16[64,2048]{1,0:T(8,128)(2,1)S(1)}, bf16[64,2048]{1,0:T(8,128)(2,1)S(1)}, u32[]{:S(2)}, u32[]{:S(2)}) %collective-permute-start.19) | collective-permute-done | bytes 262176 | tf_op jit(solution)/shard_map/ppermute | solution.py:202
  288.2 4.1 collective-permute-done.21
  294.3 3.0 place.4
  298.4 2.9 place.5
  302.4 3.2 multiply_convert_fusion
  320.2 4.6 %collective-permute-done.23.refs_2_ = bf16[4,128,256]{2,1,0:T(8,128)(2,1)} collective-permute-done((bf16[4,128,256]{2,1,0:T(8,128)(2,1)}, bf16[4,128,256]{2,1,0:T(8,128)(2,1)}, u32[]{:S(2)}, u32[]{:S(2)}) %collective-permute-start.23) | collective-permute-done | bytes 262176 | tf_op jit(solution)/shard_map/ppermute | solution.py:202
  325.4 6.9 %tiles_t.6 = bf16[32,128,256]{2,1,0:T(8,128)(2,1)} custom-call(s32[385]{0:T(512)} %concatenate.33.table, bf16[4,128,256]{2,1,0:T(8,128)(2,1)} %get-tuple-element.100.refs_0_, bf16[4,128,256]{2,1,0:T(8,128)(2,1)} %collective-permute-done.22.refs_1_, bf16[4,128,256]{2,1,0:T(8,128)(2,1)} %collective-permute-done.23.refs_2_, ...), custom_call_target="tpu_custom_call" | custom-call | tf_op jit(solution)/shard_map/tiles_t/pallas_call | solution.py:113
  334.9 7.1 %all-to-all-start.6 = ((bf16[32,128,256]{2,1,0:T(8,128)(2,1)}), bf16[32,128,256]{2,1,0:T(8,128)(2,1)S(1)}, u32[]{:S(2)}, u32[]{:S(2)}) async-start(bf16[32,128,256]{2,1,0:T(8,128)(2,1)} %tiles_t.6), calls=%async_computation.6 | async-start | bytes 4194304 | tf_op jit(solution)/shard_map/all_to_all | solution.py:22
  345.9 3.2 collective-permute-start.31
  352.9 8.6 %collective-permute-done.29 = bf16[64,2048]{1,0:T(8,128)(2,1)} collective-permute-done((bf16[64,2048]{1,0:T(8,128)(2,1)}, bf16[64,2048]{1,0:T(8,128)(2,1)}, u32[]{:S(2)}, u32[]{:S(2)}) %collective-permute-start.29) | collective-permute-done | bytes 262176 | tf_op jit(solution)/shard_map/ppermute | solution.py:202
  361.5 5.5 %collective-permute-done.31 = bf16[64,2048]{1,0:T(8,128)(2,1)} collective-permute-done((bf16[64,2048]{1,0:T(8,128)(2,1)S(1)}, bf16[64,2048]{1,0:T(8,128)(2,1)}, u32[]{:S(2)}, u32[]{:S(2)}) %collective-permute-start.31) | collective-permute-done | bytes 262176 | tf_op jit(solution)/shard_map/ppermute | solution.py:202
  374.7 6.9 %tiles_t.7 = bf16[32,128,256]{2,1,0:T(8,128)(2,1)} custom-call(s32[385]{0:T(512)} %concatenate.33.table, bf16[4,128,256]{2,1,0:T(8,128)(2,1)} %copy-done.12, bf16[4,128,256]{2,1,0:T(8,128)(2,1)} %collective-permute-done.25.refs_1_, bf16[4,128,256]{2,1,0:T(8,128)(2,1)} %collective-permute-done.26.refs_2_, bf16[4,128,256]{2,1,0:T(8,128)(2,1)} %copy-done.25, ...), custom_call_target="tpu_custom_call" | custom-call | tf_op jit(solution)/shard_map/tiles_t/pallas_call | solution.py:113
  383.0 6.1 %all-to-all-start.7 = ((bf16[32,128,256]{2,1,0:T(8,128)(2,1)}), bf16[32,128,256]{2,1,0:T(8,128)(2,1)}, u32[]{:S(2)}, u32[]{:S(2)}) async-start(bf16[32,128,256]{2,1,0:T(8,128)(2,1)} %tiles_t.7), calls=%async_computation.7 | async-start | bytes 4194304 | tf_op jit(solution)/shard_map/all_to_all | solution.py:22
  395.4 19.2 %collective-permute-done.35 = bf16[4,4096]{1,0:T(4,128)(2,1)S(1)} collective-permute-done((bf16[4,4096]{1,0:T(4,128)(2,1)S(1)}, bf16[4,4096]{1,0:T(4,128)(2,1)S(1)}, u32[]{:S(2)}, u32[]{:S(2)}) %collective-permute-start.35) | collective-permute-done | bytes 32800 | tf_op jit(solution)/shard_map/ppermute | solution.py:202
  420.3 3.0 place.6
  423.3 3.0 place.7
  (225 shorter events, 111.3 us)
Async XLA Ops:
  3.2 34.7 %all-to-all-start.1 = ((bf16[32,128,256]{2,1,0:T(8,128)(2,1)}), bf16[32,128,256]{2,1,0:T(8,128)(2,1)S(1)}, u32[]{:S(2)}, u32[]{:S(2)}) async-start(bf16[32,128,256]{2,1,0:T(8,128)(2,1)} %pick.5), calls=%async_computation.1 | async-start | bytes 4194304 | tf_op jit(solution)/shard_map/all_to_all | solution.py:22
  39.2 34.8 %all-to-all-start = ((bf16[32,128,256]{2,1,0:T(8,128)(2,1)}), bf16[32,128,256]{2,1,0:T(8,128)(2,1)}, u32[]{:S(2)}, u32[]{:S(2)}) async-start(bf16[32,128,256]{2,1,0:T(8,128)(2,1)} %pick.4), calls=%async_computation | async-start | bytes 4194304 | tf_op jit(solution)/shard_map/all_to_all | solution.py:22
  57.5 27.7 %collective-permute-start.3 = (bf16[4,128,256]{2,1,0:T(8,128)(2,1)}, bf16[4,128,256]{2,1,0:T(8,128)(2,1)S(1)}, u32[]{:S(2)}, u32[]{:S(2)}) collective-permute-start(bf16[4,128,256]{2,1,0:T(8,128)(2,1)} %get-tuple-element.40), channel_id=1, source_target_pairs={{0,64},{32,96},{64,0},{96,32},{1,65},{33,97},{65,1},{97,33},{2,66}... | collective-permute-start | bytes 786440 | tf_op jit(solution)/shard_map/ppermute | solution.py:202
  62.5 25.9 %collective-permute-start.4 = (bf16[4,128,256]{2,1,0:T(8,128)(2,1)}, bf16[4,128,256]{2,1,0:T(8,128)(2,1)S(1)}, u32[]{:S(2)}, u32[]{:S(2)}) collective-permute-start(bf16[4,128,256]{2,1,0:T(8,128)(2,1)} %get-tuple-element.41), channel_id=1, source_target_pairs={{0,32},{32,64},{64,96},{96,0},{1,33},{33,65},{65,97},{97,1},{2,34}... | collective-permute-start | bytes 786440 | tf_op jit(solution)/shard_map/ppermute | solution.py:202
  62.5 25.9 %collective-permute-start.5 = (bf16[4,128,256]{2,1,0:T(8,128)(2,1)}, bf16[4,128,256]{2,1,0:T(8,128)(2,1)S(1)}, u32[]{:S(2)}, u32[]{:S(2)}) collective-permute-start(bf16[4,128,256]{2,1,0:T(8,128)(2,1)} %get-tuple-element.42), channel_id=1, source_target_pairs={{0,96},{32,0},{64,32},{96,64},{1,97},{33,1},{65,33},{97,65},{2,98}... | collective-permute-start | bytes 786440 | tf_op jit(solution)/shard_map/ppermute | solution.py:202
  80.1 12.4 %collective-permute-start = (bf16[4,128,256]{2,1,0:T(8,128)(2,1)}, bf16[4,128,256]{2,1,0:T(8,128)(2,1)S(1)}, u32[]{:S(2)}, u32[]{:S(2)}) collective-permute-start(bf16[4,128,256]{2,1,0:T(8,128)(2,1)} %get-tuple-element.36), channel_id=1, source_target_pairs={{0,64},{32,96},{64,0},{96,32},{1,65},{33,97},{65,1},{97,33},{2,66}... | collective-permute-start | bytes 786440 | tf_op jit(solution)/shard_map/ppermute | solution.py:202
  85.2 11.2 %collective-permute-start.1 = (bf16[4,128,256]{2,1,0:T(8,128)(2,1)}, bf16[4,128,256]{2,1,0:T(8,128)(2,1)S(1)}, u32[]{:S(2)}, u32[]{:S(2)}) collective-permute-start(bf16[4,128,256]{2,1,0:T(8,128)(2,1)} %get-tuple-element.37), channel_id=1, source_target_pairs={{0,32},{32,64},{64,96},{96,0},{1,33},{33,65},{65,97},{97,1},{2,34}... | collective-permute-start | bytes 786440 | tf_op jit(solution)/shard_map/ppermute | solution.py:202
  85.2 11.6 %collective-permute-start.2 = (bf16[4,128,256]{2,1,0:T(8,128)(2,1)}, bf16[4,128,256]{2,1,0:T(8,128)(2,1)S(1)}, u32[]{:S(2)}, u32[]{:S(2)}) collective-permute-start(bf16[4,128,256]{2,1,0:T(8,128)(2,1)} %get-tuple-element.38), channel_id=1, source_target_pairs={{0,96},{32,0},{64,32},{96,64},{1,97},{33,1},{65,33},{97,65},{2,98}... | collective-permute-start | bytes 786440 | tf_op jit(solution)/shard_map/ppermute | solution.py:202
  105.9 32.6 %all-to-all-start.3 = ((bf16[32,128,256]{2,1,0:T(8,128)(2,1)}), bf16[32,128,256]{2,1,0:T(8,128)(2,1)}, u32[]{:S(2)}, u32[]{:S(2)}) async-start(bf16[32,128,256]{2,1,0:T(8,128)(2,1)} %pick.7), calls=%async_computation.3 | async-start | bytes 4194304 | tf_op jit(solution)/shard_map/all_to_all | solution.py:22
  138.5 35.1 %all-to-all-start.2 = ((bf16[32,128,256]{2,1,0:T(8,128)(2,1)}), bf16[32,128,256]{2,1,0:T(8,128)(2,1)}, u32[]{:S(2)}, u32[]{:S(2)}) async-start(bf16[32,128,256]{2,1,0:T(8,128)(2,1)} %pick.6), calls=%async_computation.2 | async-start | bytes 4194304 | tf_op jit(solution)/shard_map/all_to_all | solution.py:22
  153.8 30.0 %collective-permute-start.9 = (bf16[4,128,256]{2,1,0:T(8,128)(2,1)}, bf16[4,128,256]{2,1,0:T(8,128)(2,1)S(1)}, u32[]{:S(2)}, u32[]{:S(2)}) collective-permute-start(bf16[4,128,256]{2,1,0:T(8,128)(2,1)} %get-tuple-element.48), channel_id=1, source_target_pairs={{0,64},{32,96},{64,0},{96,32},{1,65},{33,97},{65,1},{97,33},{2,66}... | collective-permute-start | bytes 786440 | tf_op jit(solution)/shard_map/ppermute | solution.py:202
  157.9 29.3 %collective-permute-start.10 = (bf16[4,128,256]{2,1,0:T(8,128)(2,1)}, bf16[4,128,256]{2,1,0:T(8,128)(2,1)S(1)}, u32[]{:S(2)}, u32[]{:S(2)}) collective-permute-start(bf16[4,128,256]{2,1,0:T(8,128)(2,1)} %get-tuple-element.49), channel_id=1, source_target_pairs={{0,32},{32,64},{64,96},{96,0},{1,33},{33,65},{65,97},{97,1},{2,34}... | collective-permute-start | bytes 786440 | tf_op jit(solution)/shard_map/ppermute | solution.py:202
  157.9 29.3 %collective-permute-start.11 = (bf16[4,128,256]{2,1,0:T(8,128)(2,1)}, bf16[4,128,256]{2,1,0:T(8,128)(2,1)S(1)}, u32[]{:S(2)}, u32[]{:S(2)}) collective-permute-start(bf16[4,128,256]{2,1,0:T(8,128)(2,1)} %get-tuple-element.50), channel_id=1, source_target_pairs={{0,96},{32,0},{64,32},{96,64},{1,97},{33,1},{65,33},{97,65},{2,98}... | collective-permute-start | bytes 786440 | tf_op jit(solution)/shard_map/ppermute | solution.py:202
  179.7 11.5 %collective-permute-start.6 = (bf16[4,128,256]{2,1,0:T(8,128)(2,1)}, bf16[4,128,256]{2,1,0:T(8,128)(2,1)S(1)}, u32[]{:S(2)}, u32[]{:S(2)}) collective-permute-start(bf16[4,128,256]{2,1,0:T(8,128)(2,1)} %get-tuple-element.44), channel_id=1, source_target_pairs={{0,64},{32,96},{64,0},{96,32},{1,65},{33,97},{65,1},{97,33},{2,66}... | collective-permute-start | bytes 786440 | tf_op jit(solution)/shard_map/ppermute | solution.py:202
  183.8 12.0 %collective-permute-start.7 = (bf16[4,128,256]{2,1,0:T(8,128)(2,1)}, bf16[4,128,256]{2,1,0:T(8,128)(2,1)S(1)}, u32[]{:S(2)}, u32[]{:S(2)}) collective-permute-start(bf16[4,128,256]{2,1,0:T(8,128)(2,1)} %get-tuple-element.45), channel_id=1, source_target_pairs={{0,32},{32,64},{64,96},{96,0},{1,33},{33,65},{65,97},{97,1},{2,34}... | collective-permute-start | bytes 786440 | tf_op jit(solution)/shard_map/ppermute | solution.py:202
  183.8 12.0 %collective-permute-start.8 = (bf16[4,128,256]{2,1,0:T(8,128)(2,1)}, bf16[4,128,256]{2,1,0:T(8,128)(2,1)S(1)}, u32[]{:S(2)}, u32[]{:S(2)}) collective-permute-start(bf16[4,128,256]{2,1,0:T(8,128)(2,1)} %get-tuple-element.46), channel_id=1, source_target_pairs={{0,96},{32,0},{64,32},{96,64},{1,97},{33,1},{65,33},{97,65},{2,98}... | collective-permute-start | bytes 786440 | tf_op jit(solution)/shard_map/ppermute | solution.py:202
  204.6 37.4 %copy-start.13 = (bf16[4,128,256]{2,1,0:T(8,128)(2,1)}, bf16[4,128,256]{2,1,0:T(8,128)(2,1)S(1)}, u32[]{:S(2)}) copy-start(bf16[4,128,256]{2,1,0:T(8,128)(2,1)S(1)} %get-tuple-element.52.refs_0_) | copy-start | bytes 786436
  204.6 9.9 %collective-permute-start.14 = (bf16[4,128,256]{2,1,0:T(8,128)(2,1)}, bf16[4,128,256]{2,1,0:T(8,128)(2,1)}, u32[]{:S(2)}, u32[]{:S(2)}) collective-permute-start(bf16[4,128,256]{2,1,0:T(8,128)(2,1)} %get-tuple-element.102.refs_0_), channel_id=1, source_target_pairs={{0,32},{32,64},{64,96},{96,0},{1,33},{33,65},{65,97},{97,1},{2,34}... | collective-permute-start | bytes 786440 | tf_op jit(solution)/shard_map/ppermute | solution.py:202
  205.8 14.8 %collective-permute-start.13 = (bf16[4,128,256]{2,1,0:T(8,128)(2,1)}, bf16[4,128,256]{2,1,0:T(8,128)(2,1)}, u32[]{:S(2)}, u32[]{:S(2)}) collective-permute-start(bf16[4,128,256]{2,1,0:T(8,128)(2,1)} %get-tuple-element.102.refs_0_), channel_id=1, source_target_pairs={{0,64},{32,96},{64,0},{96,32},{1,65},{33,97},{65,1},{97,33},{2,66}... | collective-permute-start | bytes 786440 | tf_op jit(solution)/shard_map/ppermute | solution.py:202
  208.5 12.1 %collective-permute-start.12 = (bf16[4,128,256]{2,1,0:T(8,128)(2,1)}, bf16[4,128,256]{2,1,0:T(8,128)(2,1)}, u32[]{:S(2)}, u32[]{:S(2)}) collective-permute-start(bf16[4,128,256]{2,1,0:T(8,128)(2,1)} %get-tuple-element.102.refs_0_), channel_id=1, source_target_pairs={{0,96},{32,0},{64,32},{96,64},{1,97},{33,1},{65,33},{97,65},{2,98}... | collective-permute-start | bytes 786440 | tf_op jit(solution)/shard_map/ppermute | solution.py:202
  227.6 36.4 %all-to-all-start.4 = ((bf16[32,128,256]{2,1,0:T(8,128)(2,1)}), bf16[32,128,256]{2,1,0:T(8,128)(2,1)}, u32[]{:S(2)}, u32[]{:S(2)}) async-start(bf16[32,128,256]{2,1,0:T(8,128)(2,1)} %tiles_t.4), calls=%async_computation.4 | async-start | bytes 4194304 | tf_op jit(solution)/shard_map/all_to_all | solution.py:22
  238.9 15.2 %collective-permute-start.17 = (bf16[4,128,256]{2,1,0:T(8,128)(2,1)S(1)}, bf16[4,128,256]{2,1,0:T(8,128)(2,1)S(1)}, u32[]{:S(2)}, u32[]{:S(2)}) collective-permute-start(bf16[4,128,256]{2,1,0:T(8,128)(2,1)S(1)} %get-tuple-element.52.refs_0_), channel_id=1, source_target_pairs={{0,32},{32,64},{64,96},{96,0},{1,33},{33,65},{65,97},{97,1},{2,34}... | collective-permute-start | bytes 786440 | tf_op jit(solution)/shard_map/ppermute | solution.py:202
  239.3 14.8 %collective-permute-start.16 = (bf16[4,128,256]{2,1,0:T(8,128)(2,1)S(1)}, bf16[4,128,256]{2,1,0:T(8,128)(2,1)S(1)}, u32[]{:S(2)}, u32[]{:S(2)}) collective-permute-start(bf16[4,128,256]{2,1,0:T(8,128)(2,1)S(1)} %get-tuple-element.52.refs_0_), channel_id=1, source_target_pairs={{0,64},{32,96},{64,0},{96,32},{1,65},{33,97},{65,1},{97,33},{2,66}... | collective-permute-start | bytes 786440 | tf_op jit(solution)/shard_map/ppermute | solution.py:202
  242.0 13.5 %collective-permute-start.15 = (bf16[4,128,256]{2,1,0:T(8,128)(2,1)S(1)}, bf16[4,128,256]{2,1,0:T(8,128)(2,1)}, u32[]{:S(2)}, u32[]{:S(2)}) collective-permute-start(bf16[4,128,256]{2,1,0:T(8,128)(2,1)S(1)} %get-tuple-element.52.refs_0_), channel_id=1, source_target_pairs={{0,96},{32,0},{64,32},{96,64},{1,97},{33,1},{65,33},{97,65},{2,98}... | collective-permute-start | bytes 786440 | tf_op jit(solution)/shard_map/ppermute | solution.py:202
  262.5 12.3 %collective-permute-start.18 = (bf16[256,2048]{1,0:T(8,128)(2,1)}, bf16[256,2048]{1,0:T(8,128)(2,1)}, u32[]{:S(2)}, u32[]{:S(2)}) collective-permute-start(bf16[256,2048]{1,0:T(8,128)(2,1)} %pad_maximum_fusion), channel_id=1, source_target_pairs={{0,1},{1,0},{2,3},{3,2},{4,5},{5,4},{6,7},{7,6},{8,9},{9,8},{10,11... | collective-permute-start | bytes 3145736 | tf_op jit(solution)/shard_map/ppermute | solution.py:202
  264.0 34.4 %all-to-all-start.5 = ((bf16[32,128,256]{2,1,0:T(8,128)(2,1)}), bf16[32,128,256]{2,1,0:T(8,128)(2,1)}, u32[]{:S(2)}, u32[]{:S(2)}) async-start(bf16[32,128,256]{2,1,0:T(8,128)(2,1)} %tiles_t.5), calls=%async_computation.5 | async-start | bytes 4194304 | tf_op jit(solution)/shard_map/all_to_all | solution.py:22
  277.8 10.5 %collective-permute-start.19 = (bf16[64,2048]{1,0:T(8,128)(2,1)S(1)}, bf16[64,2048]{1,0:T(8,128)(2,1)S(1)}, u32[]{:S(2)}, u32[]{:S(2)}) collective-permute-start(bf16[64,2048]{1,0:T(8,128)(2,1)S(1)} %get-tuple-element.86), channel_id=1, source_target_pairs={{0,32},{32,64},{64,96},{96,0},{1,33},{33,65},{65,97},{97,1},{2,34}... | collective-permute-start | bytes 786440 | tf_op jit(solution)/shard_map/ppermute | solution.py:202
  278.8 13.5 %collective-permute-start.21 = (bf16[64,2048]{1,0:T(8,128)(2,1)S(1)}, bf16[64,2048]{1,0:T(8,128)(2,1)S(1)}, u32[]{:S(2)}, u32[]{:S(2)}) collective-permute-start(bf16[64,2048]{1,0:T(8,128)(2,1)S(1)} %get-tuple-element.87), channel_id=1, source_target_pairs={{0,96},{32,0},{64,32},{96,64},{1,97},{33,1},{65,33},{97,65},{2,98}... | collective-permute-start | bytes 786440 | tf_op jit(solution)/shard_map/ppermute | solution.py:202
  281.1 12.0 %collective-permute-start.20 = (bf16[64,2048]{1,0:T(8,128)(2,1)S(1)}, bf16[64,2048]{1,0:T(8,128)(2,1)}, u32[]{:S(2)}, u32[]{:S(2)}) collective-permute-start(bf16[64,2048]{1,0:T(8,128)(2,1)S(1)} %get-tuple-element.88), channel_id=1, source_target_pairs={{0,64},{32,96},{64,0},{96,32},{1,65},{33,97},{65,1},{97,33},{2,66}... | collective-permute-start | bytes 786440 | tf_op jit(solution)/shard_map/ppermute | solution.py:202
  308.6 52.9 %copy-start.12 = (bf16[4,128,256]{2,1,0:T(8,128)(2,1)}, bf16[4,128,256]{2,1,0:T(8,128)(2,1)S(1)}, u32[]{:S(2)}) copy-start(bf16[4,128,256]{2,1,0:T(8,128)(2,1)S(1)} %get-tuple-element.60.refs_0_) | copy-start | bytes 786436
  308.6 11.6 %collective-permute-start.24 = (bf16[4,128,256]{2,1,0:T(8,128)(2,1)}, bf16[4,128,256]{2,1,0:T(8,128)(2,1)}, u32[]{:S(2)}, u32[]{:S(2)}) collective-permute-start(bf16[4,128,256]{2,1,0:T(8,128)(2,1)} %get-tuple-element.100.refs_0_), channel_id=1, source_target_pairs={{0,32},{32,64},{64,96},{96,0},{1,33},{33,65},{65,97},{97,1},{2,34}... | collective-permute-start | bytes 786440 | tf_op jit(solution)/shard_map/ppermute | solution.py:202
  309.6 15.2 %collective-permute-start.23 = (bf16[4,128,256]{2,1,0:T(8,128)(2,1)}, bf16[4,128,256]{2,1,0:T(8,128)(2,1)}, u32[]{:S(2)}, u32[]{:S(2)}) collective-permute-start(bf16[4,128,256]{2,1,0:T(8,128)(2,1)} %get-tuple-element.100.refs_0_), channel_id=1, source_target_pairs={{0,64},{32,96},{64,0},{96,32},{1,65},{33,97},{65,1},{97,33},{2,66}... | collective-permute-start | bytes 786440 | tf_op jit(solution)/shard_map/ppermute | solution.py:202
  311.9 13.5 %collective-permute-start.22 = (bf16[4,128,256]{2,1,0:T(8,128)(2,1)}, bf16[4,128,256]{2,1,0:T(8,128)(2,1)}, u32[]{:S(2)}, u32[]{:S(2)}) collective-permute-start(bf16[4,128,256]{2,1,0:T(8,128)(2,1)} %get-tuple-element.100.refs_0_), channel_id=1, source_target_pairs={{0,96},{32,0},{64,32},{96,64},{1,97},{33,1},{65,33},{97,65},{2,98}... | collective-permute-start | bytes 786440 | tf_op jit(solution)/shard_map/ppermute | solution.py:202
  332.3 9.7 %collective-permute-start.28 = (bf16[256,2048]{1,0:T(8,128)(2,1)}, bf16[256,2048]{1,0:T(8,128)(2,1)}, u32[]{:S(2)}, u32[]{:S(2)}) collective-permute-start(bf16[256,2048]{1,0:T(8,128)(2,1)} %pad_maximum_fusion.1), channel_id=1, source_target_pairs={{0,1},{1,0},{2,3},{3,2},{4,5},{5,4},{6,7},{7,6},{8,9},{9,8},{10,11... | collective-permute-start | bytes 3145736 | tf_op jit(solution)/shard_map/ppermute | solution.py:202
  334.9 46.7 %all-to-all-start.6 = ((bf16[32,128,256]{2,1,0:T(8,128)(2,1)}), bf16[32,128,256]{2,1,0:T(8,128)(2,1)S(1)}, u32[]{:S(2)}, u32[]{:S(2)}) async-start(bf16[32,128,256]{2,1,0:T(8,128)(2,1)} %tiles_t.6), calls=%async_computation.6 | async-start | bytes 4194304 | tf_op jit(solution)/shard_map/all_to_all | solution.py:22
  345.9 15.6 %collective-permute-start.29 = (bf16[64,2048]{1,0:T(8,128)(2,1)}, bf16[64,2048]{1,0:T(8,128)(2,1)}, u32[]{:S(2)}, u32[]{:S(2)}) collective-permute-start(bf16[64,2048]{1,0:T(8,128)(2,1)} %get-tuple-element.83), channel_id=1, source_target_pairs={{0,32},{32,64},{64,96},{96,0},{1,33},{33,65},{65,97},{97,1},{2,34}... | collective-permute-start | bytes 786440 | tf_op jit(solution)/shard_map/ppermute | solution.py:202
  345.9 21.2 %collective-permute-start.31 = (bf16[64,2048]{1,0:T(8,128)(2,1)S(1)}, bf16[64,2048]{1,0:T(8,128)(2,1)}, u32[]{:S(2)}, u32[]{:S(2)}) collective-permute-start(bf16[64,2048]{1,0:T(8,128)(2,1)S(1)} %get-tuple-element.84), channel_id=1, source_target_pairs={{0,96},{32,0},{64,32},{96,64},{1,97},{33,1},{65,33},{97,65},{2,98}... | collective-permute-start | bytes 786440 | tf_op jit(solution)/shard_map/ppermute | solution.py:202
  349.1 17.9 %collective-permute-start.30 = (bf16[64,2048]{1,0:T(8,128)(2,1)S(1)}, bf16[64,2048]{1,0:T(8,128)(2,1)}, u32[]{:S(2)}, u32[]{:S(2)}) collective-permute-start(bf16[64,2048]{1,0:T(8,128)(2,1)S(1)} %get-tuple-element.85), channel_id=1, source_target_pairs={{0,64},{32,96},{64,0},{96,32},{1,65},{33,97},{65,1},{97,33},{2,66}... | collective-permute-start | bytes 786440 | tf_op jit(solution)/shard_map/ppermute | solution.py:202
  350.0 21.6 %collective-permute-start.27 = (bf16[4,128,256]{2,1,0:T(8,128)(2,1)S(1)}, bf16[4,128,256]{2,1,0:T(8,128)(2,1)S(1)}, u32[]{:S(2)}, u32[]{:S(2)}) collective-permute-start(bf16[4,128,256]{2,1,0:T(8,128)(2,1)S(1)} %get-tuple-element.60.refs_0_), channel_id=1, source_target_pairs={{0,32},{32,64},{64,96},{96,0},{1,33},{33,65},{65,97},{97,1},{2,34}... | collective-permute-start | bytes 786440 | tf_op jit(solution)/shard_map/ppermute | solution.py:202
  351.4 23.3 %collective-permute-start.26 = (bf16[4,128,256]{2,1,0:T(8,128)(2,1)S(1)}, bf16[4,128,256]{2,1,0:T(8,128)(2,1)}, u32[]{:S(2)}, u32[]{:S(2)}) collective-permute-start(bf16[4,128,256]{2,1,0:T(8,128)(2,1)S(1)} %get-tuple-element.60.refs_0_), channel_id=1, source_target_pairs={{0,64},{32,96},{64,0},{96,32},{1,65},{33,97},{65,1},{97,33},{2,66}... | collective-permute-start | bytes 786440 | tf_op jit(solution)/shard_map/ppermute | solution.py:202
  361.5 13.2 %collective-permute-start.25 = (bf16[4,128,256]{2,1,0:T(8,128)(2,1)S(1)}, bf16[4,128,256]{2,1,0:T(8,128)(2,1)}, u32[]{:S(2)}, u32[]{:S(2)}) collective-permute-start(bf16[4,128,256]{2,1,0:T(8,128)(2,1)S(1)} %get-tuple-element.60.refs_0_), channel_id=1, source_target_pairs={{0,96},{32,0},{64,32},{96,64},{1,97},{33,1},{65,33},{97,65},{2,98}... | collective-permute-start | bytes 786440 | tf_op jit(solution)/shard_map/ppermute | solution.py:202
  369.2 19.9 %collective-permute-start.32 = (bf16[16,4096]{1,0:T(8,128)(2,1)}, bf16[16,4096]{1,0:T(8,128)(2,1)}, u32[]{:S(2)}, u32[]{:S(2)}) collective-permute-start(bf16[16,4096]{1,0:T(8,128)(2,1)} %get-tuple-element.89), channel_id=1, source_target_pairs={{0,8},{8,16},{16,24},{24,0},{1,9},{9,17},{17,25},{25,1},{2,10},{10... | collective-permute-start | bytes 393224 | tf_op jit(solution)/shard_map/ppermute | solution.py:202
  370.7 18.4 %collective-permute-start.33 = (bf16[16,4096]{1,0:T(8,128)(2,1)}, bf16[16,4096]{1,0:T(8,128)(2,1)}, u32[]{:S(2)}, u32[]{:S(2)}) collective-permute-start(bf16[16,4096]{1,0:T(8,128)(2,1)} %get-tuple-element.90), channel_id=1, source_target_pairs={{0,16},{8,24},{16,0},{24,8},{1,17},{9,25},{17,1},{25,9},{2,18},{10... | collective-permute-start | bytes 393224 | tf_op jit(solution)/shard_map/ppermute | solution.py:202
  372.2 16.9 %collective-permute-start.34 = (bf16[16,4096]{1,0:T(8,128)(2,1)S(1)}, bf16[16,4096]{1,0:T(8,128)(2,1)}, u32[]{:S(2)}, u32[]{:S(2)}) collective-permute-start(bf16[16,4096]{1,0:T(8,128)(2,1)S(1)} %get-tuple-element.91), channel_id=1, source_target_pairs={{0,24},{8,0},{16,8},{24,16},{1,25},{9,1},{17,9},{25,17},{2,26},{10... | collective-permute-start | bytes 393224 | tf_op jit(solution)/shard_map/ppermute | solution.py:202
  383.0 40.3 %all-to-all-start.7 = ((bf16[32,128,256]{2,1,0:T(8,128)(2,1)}), bf16[32,128,256]{2,1,0:T(8,128)(2,1)}, u32[]{:S(2)}, u32[]{:S(2)}) async-start(bf16[32,128,256]{2,1,0:T(8,128)(2,1)} %tiles_t.7), calls=%async_computation.7 | async-start | bytes 4194304 | tf_op jit(solution)/shard_map/all_to_all | solution.py:22
  390.3 24.3 %collective-permute-start.35 = (bf16[4,4096]{1,0:T(4,128)(2,1)S(1)}, bf16[4,4096]{1,0:T(4,128)(2,1)S(1)}, u32[]{:S(2)}, u32[]{:S(2)}) collective-permute-start(bf16[4,4096]{1,0:T(4,128)(2,1)S(1)} %get-tuple-element.104), channel_id=1, source_target_pairs={{0,2},{2,4},{4,6},{6,0},{1,3},{3,5},{5,7},{7,1},{8,10},{10,12},{12... | collective-permute-start | bytes 98312 | tf_op jit(solution)/shard_map/ppermute | solution.py:202
  391.8 24.5 %collective-permute-start.37 = (bf16[4,4096]{1,0:T(4,128)(2,1)S(1)}, bf16[4,4096]{1,0:T(4,128)(2,1)S(1)}, u32[]{:S(2)}, u32[]{:S(2)}) collective-permute-start(bf16[4,4096]{1,0:T(4,128)(2,1)S(1)} %get-tuple-element.105), channel_id=1, source_target_pairs={{0,6},{2,0},{4,2},{6,4},{1,7},{3,1},{5,3},{7,5},{8,14},{10,8},{12,... | collective-permute-start | bytes 98312 | tf_op jit(solution)/shard_map/ppermute | solution.py:202
  393.6 25.2 %collective-permute-start.36 = (bf16[4,4096]{1,0:T(4,128)(2,1)S(1)}, bf16[4,4096]{1,0:T(4,128)(2,1)S(1)}, u32[]{:S(2)}, u32[]{:S(2)}) collective-permute-start(bf16[4,4096]{1,0:T(4,128)(2,1)S(1)} %get-tuple-element.106), channel_id=1, source_target_pairs={{0,4},{2,6},{4,0},{6,2},{1,5},{3,7},{5,1},{7,3},{8,12},{10,14},{12... | collective-permute-start | bytes 98312 | tf_op jit(solution)/shard_map/ppermute | solution.py:202
  (37 other events, 236.5 us)
where the time goes:
time: 437 us; the launch traced here: 428 us
  waiting for transfers between devices  155 us (35%)
  starting transfers between devices  123 us (28%)
  Pallas kernels  74.6 us (17%)
  matrix products  25 us (6%)
  local copies, waits for them, and re-layouts  23.8 us (5%)
  other arithmetic  23.2 us (5%)
    ppermute x38, waiting for transfers between devices, shifted(): lax.ppermute(value, axis, [(i, (i + step) % length) for i in range(length)])  89 us
    all_to_all x8, waiting for transfers between devices, exchange(): return lax.all_to_all(value, axis, split_axis=0, concat_axis=0, tiled=True)  66.2 us
    ppermute x38, starting transfers between devices, shifted(): lax.ppermute(value, axis, [(i, (i + step) % length) for i in range(length)])  63.5 us
    all_to_all x8, starting transfers between devices, exchange(): return lax.all_to_all(value, axis, split_axis=0, concat_axis=0, tiled=True)  59.2 us
    pallas_call x8, Pallas kernels, run_tiles(): pl.pallas_call(functools.partial(tiles_kernel, steps=steps, transposed=tr...  52.3 us
    pallas_call x4, Pallas kernels, place_blocks(): pl.pallas_call(place_kernel, grid=(1,), out_shape=jax.ShapeDtypeStruct(bl...  11.9 us
    unnamed x78, local copies, waits for them, and re-layouts  11.5 us
    pallas_call x4, Pallas kernels, pick_blocks(): pl.pallas_call(pick_kernel, grid=(1,), out_shape=jax.ShapeDtypeStruct((co...  10.4 us
  transfers between devices with their start and end apart: 46, of which 23 were waited for; matrix products, arithmetic and copies ran while one was open for 9% of the time, Pallas kernels for 12%

commit v1 on v0

--- a/solution.py
+++ b/solution.py
@@ -228,19 +228,24 @@
 
 def reduce_weights(units, d_pre, activated, grad, unit_order, act_order, after):
     contract_rows = (((0,), (0,)), ((), ()))
-    ordered_units = jnp.dot(units, unit_order).reshape(units.shape[0], 2, 1, -1)
-    ordered_acts = jnp.dot(activated, act_order).reshape(units.shape[0], 2, 2, -1)
-    halves = []
-    for half in range(2):
-        terms = [
-            lax.dot_general(left, right, contract_rows, preferred_element_type=jnp.float32)
-            for left, right in (
-                (ordered_units[:, half, 0], d_pre),
-                (ordered_acts[:, half, 0], grad),
-                (ordered_acts[:, half, 1], grad),
-            )
-        ]
-        halves.append(jnp.concatenate([term.astype(jnp.bfloat16) for term in terms], axis=1))
+    in_term, out_term = [
+        lax.dot_general(
+            jnp.dot(left, order), right, contract_rows, preferred_element_type=jnp.float32
+        ).astype(jnp.bfloat16)
+        for left, order, right in ((units, unit_order, d_pre), (activated, act_order, grad))
+    ]
+    quarter = out_term.shape[0] // 4
+    halves = [
+        jnp.concatenate(
+            [
+                in_term[half * quarter : (half + 1) * quarter],
+                out_term[2 * half * quarter : (2 * half + 1) * quarter],
+                out_term[(2 * half + 1) * quarter : (2 * half + 2) * quarter],
+            ],
+            axis=1,
+        )
+        for half in range(2)
+    ]
     halves[1], _ = lax.optimization_barrier((halves[1], after))
     total = halves[0].astype(jnp.float32) + shifted(halves[1], NEAR, 1).astype(jnp.float32)
     return scatter_sum(total, FAR[0])

time: 437 us -> 432 us (0.989); the launches traced: 428 us -> 432 us
  waiting for transfers between devices: 155 us -> 169 us
    all_to_all x8, waiting for transfers between devices: 66.2 us -> 74.7 us  [exchange(): return lax.all_to_all(value, axis, split_axis=0, concat_axis=0, tiled=True)]
    ppermute x38, starting transfers between devices: 63.5 us -> 57.5 us  [shifted(): lax.ppermute(value, axis, [(i, (i + step) % length) for i in range(length)])]
    ppermute x38, waiting for transfers between devices: 89 us -> 94.3 us  [shifted(): lax.ppermute(value, axis, [(i, (i + step) % length) for i in range(length)])]
    unnamed x78 -> x66, local copies, waits for them, and re-layouts: 11.5 us -> 10.2 us
    dot_general x16 -> x4, matrix products: 14.3 us -> 13.1 us  [reduce_weights(): lax.dot_general(jnp.dot(left, order), right, contract_rows, preferred_ele...]
  transfers between devices with their start and end apart: 46 -> 46, of which waited for: 23 -> 23; matrix products, arithmetic and copies ran while one was open for 9% -> 9% of each run, Pallas kernels for 12% -> 11%
where the time goes in v1:
time: 432 us
  waiting for transfers between devices  169 us (39%)
  starting transfers between devices  119 us (28%)
  Pallas kernels  72.5 us (17%)
  matrix products  24.8 us (6%)
  other arithmetic  23.3 us (5%)
  local copies, waits for them, and re-layouts  19.8 us (5%)
    ppermute x38, waiting for transfers between devices, shifted(): lax.ppermute(value, axis, [(i, (i + step) % length) for i in range(length)])  94.3 us
    all_to_all x8, waiting for transfers between devices, exchange(): return lax.all_to_all(value, axis, split_axis=0, concat_axis=0, tiled=True)  74.7 us
    all_to_all x8, starting transfers between devices, exchange(): return lax.all_to_all(value, axis, split_axis=0, concat_axis=0, tiled=True)  61.9 us
    ppermute x38, starting transfers between devices, shifted(): lax.ppermute(value, axis, [(i, (i + step) % length) for i in range(length)])  57.5 us
    pallas_call x8, Pallas kernels, run_tiles(): pl.pallas_call(functools.partial(tiles_kernel, steps=steps, transposed=tr...  50.2 us
    dot_general x4, matrix products, reduce_weights(): lax.dot_general(jnp.dot(left, order), right, contract_rows, preferred_ele...  13.1 us
    pallas_call x4, Pallas kernels, place_blocks(): pl.pallas_call(place_kernel, grid=(1,), out_shape=jax.ShapeDtypeStruct(bl...  11.9 us
    pallas_call x4, Pallas kernels, pick_blocks(): pl.pallas_call(pick_kernel, grid=(1,), out_shape=jax.ShapeDtypeStruct((co...  10.4 us
  transfers between devices with their start and end apart: 46, of which 23 were waited for; matrix products, arithmetic and copies ran while one was open for 9% of the time, Pallas kernels for 11%

profile of v1, /device:TPU:32, one launch (start us, length us, event | category | flops | bytes accessed | tf_op | source)
XLA Modules:
  0.0 432.2 jit_solution(8337085483766605212)
XLA Ops:
  0.6 2.6 pick.5
  3.2 8.1 %all-to-all-start.1 = ((bf16[32,128,256]{2,1,0:T(8,128)(2,1)}), bf16[32,128,256]{2,1,0:T(8,128)(2,1)S(1)}, u32[]{:S(2)}, u32[]{:S(2)}) async-start(bf16[32,128,256]{2,1,0:T(8,128)(2,1)} %pick.5), calls=%async_computation.1 | async-start | bytes 4194304 | tf_op jit(solution)/shard_map/all_to_all | solution.py:22
  15.7 22.2 %all-to-all-done.1.refs_0_ = bf16[32,128,256]{2,1,0:T(8,128)(2,1)S(1)} async-done(((bf16[32,128,256]{2,1,0:T(8,128)(2,1)}), bf16[32,128,256]{2,1,0:T(8,128)(2,1)S(1)}, u32[]{:S(2)}, u32[]{:S(2)}) %all-to-all-start.1) | async-done | bytes 2097184 | tf_op jit(solution)/shard_map/all_to_all | solution.py:22
  39.3 8.1 %all-to-all-start = ((bf16[32,128,256]{2,1,0:T(8,128)(2,1)}), bf16[32,128,256]{2,1,0:T(8,128)(2,1)}, u32[]{:S(2)}, u32[]{:S(2)}) async-start(bf16[32,128,256]{2,1,0:T(8,128)(2,1)} %pick.4), calls=%async_computation | async-start | bytes 4194304 | tf_op jit(solution)/shard_map/all_to_all | solution.py:22
  51.4 5.8 %tiles.5 = (bf16[4,128,256]{2,1,0:T(8,128)(2,1)}, bf16[4,128,256]{2,1,0:T(8,128)(2,1)}, bf16[4,128,256]{2,1,0:T(8,128)(2,1)}, bf16[4,128,256]{2,1,0:T(8,128)(2,1)}) custom-call(s32[337]{0:T(512)} %concatenate.34.table, bf16[32,128,256]{2,1,0:T(8,128)(2,1)} %copy-done.2, bf16[96,128,128]{2,1,0:T(8,128)(2,1)} %refs_4_.7), custom_call_target="tpu_custom_call" | custom-call | tf_op jit(solution)/shard_map/tiles/pallas_call | solution.py:113
  57.2 3.5 collective-permute-start.3
  64.0 10.0 %all-to-all-done.refs_0_ = bf16[32,128,256]{2,1,0:T(8,128)(2,1)} async-done(((bf16[32,128,256]{2,1,0:T(8,128)(2,1)}), bf16[32,128,256]{2,1,0:T(8,128)(2,1)}, u32[]{:S(2)}, u32[]{:S(2)}) %all-to-all-start) | async-done | bytes 2097184 | tf_op jit(solution)/shard_map/all_to_all | solution.py:22
  74.0 5.9 %tiles.4 = (bf16[4,128,256]{2,1,0:T(8,128)(2,1)}, bf16[4,128,256]{2,1,0:T(8,128)(2,1)}, bf16[4,128,256]{2,1,0:T(8,128)(2,1)}, bf16[4,128,256]{2,1,0:T(8,128)(2,1)}) custom-call(s32[337]{0:T(512)} %concatenate.34.table, bf16[32,128,256]{2,1,0:T(8,128)(2,1)} %all-to-all-done.refs_0_, bf16[96,128,128]{2,1,0:T(8,128)(2,1)} %refs_4_.7), custom_call_target="tpu_custom_call" | custom-call | tf_op jit(solution)/shard_map/tiles/pallas_call | solution.py:113
  79.9 3.5 collective-permute-start
  86.8 3.7 collective-permute-done
  90.5 6.0 %collective-permute-done.1 = bf16[4,128,256]{2,1,0:T(8,128)(2,1)S(1)} collective-permute-done((bf16[4,128,256]{2,1,0:T(8,128)(2,1)}, bf16[4,128,256]{2,1,0:T(8,128)(2,1)S(1)}, u32[]{:S(2)}, u32[]{:S(2)}) %collective-permute-start.1) | collective-permute-done | bytes 262176 | tf_op jit(solution)/shard_map/ppermute | solution.py:202
  105.6 6.3 %all-to-all-start.3 = ((bf16[32,128,256]{2,1,0:T(8,128)(2,1)}), bf16[32,128,256]{2,1,0:T(8,128)(2,1)}, u32[]{:S(2)}, u32[]{:S(2)}) async-start(bf16[32,128,256]{2,1,0:T(8,128)(2,1)} %pick.7), calls=%async_computation.3 | async-start | bytes 4194304 | tf_op jit(solution)/shard_map/all_to_all | solution.py:22
  112.0 2.6 pick.6
  114.6 23.7 %all-to-all-done.3.refs_0_ = bf16[32,128,256]{2,1,0:T(8,128)(2,1)} async-done(((bf16[32,128,256]{2,1,0:T(8,128)(2,1)}), bf16[32,128,256]{2,1,0:T(8,128)(2,1)}, u32[]{:S(2)}, u32[]{:S(2)}) %all-to-all-start.3) | async-done | bytes 2097184 | tf_op jit(solution)/shard_map/all_to_all | solution.py:22
  138.3 8.4 %all-to-all-start.2 = ((bf16[32,128,256]{2,1,0:T(8,128)(2,1)}), bf16[32,128,256]{2,1,0:T(8,128)(2,1)}, u32[]{:S(2)}, u32[]{:S(2)}) async-start(bf16[32,128,256]{2,1,0:T(8,128)(2,1)} %pick.6), calls=%async_computation.2 | async-start | bytes 4194304 | tf_op jit(solution)/shard_map/all_to_all | solution.py:22
  146.7 5.9 %tiles.7 = (bf16[4,128,256]{2,1,0:T(8,128)(2,1)}, bf16[4,128,256]{2,1,0:T(8,128)(2,1)}, bf16[4,128,256]{2,1,0:T(8,128)(2,1)}, bf16[4,128,256]{2,1,0:T(8,128)(2,1)}) custom-call(s32[337]{0:T(512)} %concatenate.34.table, bf16[32,128,256]{2,1,0:T(8,128)(2,1)} %all-to-all-done.3.refs_0_, bf16[96,128,128]{2,1,0:T(8,128)(2,1)} %refs_4_.7), custom_call_target="tpu_custom_call" | custom-call | tf_op jit(solution)/shard_map/tiles/pallas_call | solution.py:113
  158.3 15.1 %all-to-all-done.2.refs_0_ = bf16[32,128,256]{2,1,0:T(8,128)(2,1)} async-done(((bf16[32,128,256]{2,1,0:T(8,128)(2,1)}), bf16[32,128,256]{2,1,0:T(8,128)(2,1)}, u32[]{:S(2)}, u32[]{:S(2)}) %all-to-all-start.2) | async-done | bytes 2097184 | tf_op jit(solution)/shard_map/all_to_all | solution.py:22
  173.4 5.9 %tiles.6 = (bf16[4,128,256]{2,1,0:T(8,128)(2,1)}, bf16[4,128,256]{2,1,0:T(8,128)(2,1)}, bf16[4,128,256]{2,1,0:T(8,128)(2,1)}, bf16[4,128,256]{2,1,0:T(8,128)(2,1)}) custom-call(s32[337]{0:T(512)} %concatenate.34.table, bf16[32,128,256]{2,1,0:T(8,128)(2,1)} %all-to-all-done.2.refs_0_, bf16[96,128,128]{2,1,0:T(8,128)(2,1)} %refs_4_.7), custom_call_target="tpu_custom_call" | custom-call | tf_op jit(solution)/shard_map/tiles/pallas_call | solution.py:113
  185.1 3.8 collective-permute-done.6
  188.9 7.0 %collective-permute-done.7 = bf16[4,128,256]{2,1,0:T(8,128)(2,1)S(1)} collective-permute-done((bf16[4,128,256]{2,1,0:T(8,128)(2,1)}, bf16[4,128,256]{2,1,0:T(8,128)(2,1)S(1)}, u32[]{:S(2)}, u32[]{:S(2)}) %collective-permute-start.7) | collective-permute-done | bytes 262176 | tf_op jit(solution)/shard_map/ppermute | solution.py:202
  205.1 2.8 collective-permute-start.13
  210.8 3.2 collective-permute-done.14.refs_3_
  214.0 5.9 %collective-permute-done.13.refs_2_ = bf16[4,128,256]{2,1,0:T(8,128)(2,1)} collective-permute-done((bf16[4,128,256]{2,1,0:T(8,128)(2,1)S(1)}, bf16[4,128,256]{2,1,0:T(8,128)(2,1)}, u32[]{:S(2)}, u32[]{:S(2)}) %collective-permute-start.13) | collective-permute-done | bytes 262176 | tf_op jit(solution)/shard_map/ppermute | solution.py:202
  220.0 6.7 %tiles_t.4 = bf16[32,128,256]{2,1,0:T(8,128)(2,1)} custom-call(s32[385]{0:T(512)} %concatenate.33.table, bf16[4,128,256]{2,1,0:T(8,128)(2,1)} %copy-done.12, bf16[4,128,256]{2,1,0:T(8,128)(2,1)} %collective-permute-done.12.refs_1_, bf16[4,128,256]{2,1,0:T(8,128)(2,1)} %collective-permute-done.13.refs_2_, bf16[4,128,256]{2,1,0:T(8,128)(2,1)} %copy-done.18, ...), custom_call_target="tpu_custom_call" | custom-call | tf_op jit(solution)/shard_map/tiles_t/pallas_call | solution.py:113
  226.6 8.2 %all-to-all-start.4 = ((bf16[32,128,256]{2,1,0:T(8,128)(2,1)}), bf16[32,128,256]{2,1,0:T(8,128)(2,1)}, u32[]{:S(2)}, u32[]{:S(2)}) async-start(bf16[32,128,256]{2,1,0:T(8,128)(2,1)} %tiles_t.4), calls=%async_computation.4 | async-start | bytes 4194304 | tf_op jit(solution)/shard_map/all_to_all | solution.py:22
  234.8 3.4 convolution_convert_fusion.3
  239.5 4.1 convolution_convert_fusion.2
  250.0 8.7 %collective-permute-done.17.refs_3_ = bf16[4,128,256]{2,1,0:T(8,128)(2,1)S(1)} collective-permute-done((bf16[4,128,256]{2,1,0:T(8,128)(2,1)S(1)}, bf16[4,128,256]{2,1,0:T(8,128)(2,1)S(1)}, u32[]{:S(2)}, u32[]{:S(2)}) %collective-permute-start.17) | collective-permute-done | bytes 262176 | tf_op jit(solution)/shard_map/ppermute | solution.py:202
  260.2 6.7 %tiles_t.5 = bf16[32,128,256]{2,1,0:T(8,128)(2,1)} custom-call(s32[385]{0:T(512)} %concatenate.33.table, bf16[4,128,256]{2,1,0:T(8,128)(2,1)} %copy-done.11, bf16[4,128,256]{2,1,0:T(8,128)(2,1)} %collective-permute-done.15.refs_1_, bf16[4,128,256]{2,1,0:T(8,128)(2,1)} %copy-done.20, bf16[4,128,256]{2,1,0:T(8,128)(2,1)} %copy-done.19, ...), custom_call_target="tpu_custom_call" | custom-call | tf_op jit(solution)/shard_map/tiles_t/pallas_call | solution.py:113
  267.9 8.0 %all-to-all-start.5 = ((bf16[32,128,256]{2,1,0:T(8,128)(2,1)}), bf16[32,128,256]{2,1,0:T(8,128)(2,1)}, u32[]{:S(2)}, u32[]{:S(2)}) async-start(bf16[32,128,256]{2,1,0:T(8,128)(2,1)} %tiles_t.5), calls=%async_computation.5 | async-start | bytes 4194304 | tf_op jit(solution)/shard_map/all_to_all | solution.py:22
  279.1 3.2 collective-permute-start.21
  282.3 11.9 %collective-permute-done.19 = bf16[64,2048]{1,0:T(8,128)(2,1)S(1)} collective-permute-done((bf16[64,2048]{1,0:T(8,128)(2,1)S(1)}, bf16[64,2048]{1,0:T(8,128)(2,1)S(1)}, u32[]{:S(2)}, u32[]{:S(2)}) %collective-permute-start.19) | collective-permute-done | bytes 262176 | tf_op jit(solution)/shard_map/ppermute | solution.py:202
  295.5 3.0 place.4
  298.4 3.8 all-to-all-done.5.returned
  302.2 2.9 place.5
  306.2 3.2 multiply_convert_fusion
  319.2 3.1 convolution_convert_fusion
  324.3 4.4 %collective-permute-done.24.refs_3_ = bf16[4,128,256]{2,1,0:T(8,128)(2,1)} collective-permute-done((bf16[4,128,256]{2,1,0:T(8,128)(2,1)}, bf16[4,128,256]{2,1,0:T(8,128)(2,1)}, u32[]{:S(2)}, u32[]{:S(2)}) %collective-permute-start.24) | collective-permute-done | bytes 262176 | tf_op jit(solution)/shard_map/ppermute | solution.py:202
  329.4 6.6 %tiles_t.6 = bf16[32,128,256]{2,1,0:T(8,128)(2,1)} custom-call(s32[385]{0:T(512)} %concatenate.33.table, bf16[4,128,256]{2,1,0:T(8,128)(2,1)} %get-tuple-element.104.refs_0_, bf16[4,128,256]{2,1,0:T(8,128)(2,1)} %collective-permute-done.22.refs_1_, bf16[4,128,256]{2,1,0:T(8,128)(2,1)} %collective-permute-done.23.refs_2_, ...), custom_call_target="tpu_custom_call" | custom-call | tf_op jit(solution)/shard_map/tiles_t/pallas_call | solution.py:113
  337.6 6.8 %all-to-all-start.6 = ((bf16[32,128,256]{2,1,0:T(8,128)(2,1)}), bf16[32,128,256]{2,1,0:T(8,128)(2,1)S(1)}, u32[]{:S(2)}, u32[]{:S(2)}) async-start(bf16[32,128,256]{2,1,0:T(8,128)(2,1)} %tiles_t.6), calls=%async_computation.6 | async-start | bytes 4194304 | tf_op jit(solution)/shard_map/all_to_all | solution.py:22
  348.3 3.2 collective-permute-start.31
  355.1 9.5 %collective-permute-done.29 = bf16[64,2048]{1,0:T(8,128)(2,1)} collective-permute-done((bf16[64,2048]{1,0:T(8,128)(2,1)}, bf16[64,2048]{1,0:T(8,128)(2,1)}, u32[]{:S(2)}, u32[]{:S(2)}) %collective-permute-start.29) | collective-permute-done | bytes 262176 | tf_op jit(solution)/shard_map/ppermute | solution.py:202
  364.6 4.8 %collective-permute-done.31 = bf16[64,2048]{1,0:T(8,128)(2,1)} collective-permute-done((bf16[64,2048]{1,0:T(8,128)(2,1)S(1)}, bf16[64,2048]{1,0:T(8,128)(2,1)}, u32[]{:S(2)}, u32[]{:S(2)}) %collective-permute-start.31) | collective-permute-done | bytes 262176 | tf_op jit(solution)/shard_map/ppermute | solution.py:202
  377.1 6.6 %tiles_t.7 = bf16[32,128,256]{2,1,0:T(8,128)(2,1)} custom-call(s32[385]{0:T(512)} %concatenate.33.table, bf16[4,128,256]{2,1,0:T(8,128)(2,1)} %copy-done.10, bf16[4,128,256]{2,1,0:T(8,128)(2,1)} %collective-permute-done.25.refs_1_, bf16[4,128,256]{2,1,0:T(8,128)(2,1)} %collective-permute-done.26.refs_2_, bf16[4,128,256]{2,1,0:T(8,128)(2,1)} %copy-done.17, ...), custom_call_target="tpu_custom_call" | custom-call | tf_op jit(solution)/shard_map/tiles_t/pallas_call | solution.py:113
  385.1 8.1 %all-to-all-start.7 = ((bf16[32,128,256]{2,1,0:T(8,128)(2,1)}), bf16[32,128,256]{2,1,0:T(8,128)(2,1)}, u32[]{:S(2)}, u32[]{:S(2)}) async-start(bf16[32,128,256]{2,1,0:T(8,128)(2,1)} %tiles_t.7), calls=%async_computation.7 | async-start | bytes 4194304 | tf_op jit(solution)/shard_map/all_to_all | solution.py:22
  399.5 19.2 %collective-permute-done.35 = bf16[4,4096]{1,0:T(4,128)(2,1)S(1)} collective-permute-done((bf16[4,4096]{1,0:T(4,128)(2,1)S(1)}, bf16[4,4096]{1,0:T(4,128)(2,1)S(1)}, u32[]{:S(2)}, u32[]{:S(2)}) %collective-permute-start.35) | collective-permute-done | bytes 32800 | tf_op jit(solution)/shard_map/ppermute | solution.py:202
  424.4 3.0 place.6
  427.4 3.0 place.7
  (201 shorter events, 106.5 us)
Async XLA Ops:
  3.2 34.7 %all-to-all-start.1 = ((bf16[32,128,256]{2,1,0:T(8,128)(2,1)}), bf16[32,128,256]{2,1,0:T(8,128)(2,1)S(1)}, u32[]{:S(2)}, u32[]{:S(2)}) async-start(bf16[32,128,256]{2,1,0:T(8,128)(2,1)} %pick.5), calls=%async_computation.1 | async-start | bytes 4194304 | tf_op jit(solution)/shard_map/all_to_all | solution.py:22
  39.3 34.8 %all-to-all-start = ((bf16[32,128,256]{2,1,0:T(8,128)(2,1)}), bf16[32,128,256]{2,1,0:T(8,128)(2,1)}, u32[]{:S(2)}, u32[]{:S(2)}) async-start(bf16[32,128,256]{2,1,0:T(8,128)(2,1)} %pick.4), calls=%async_computation | async-start | bytes 4194304 | tf_op jit(solution)/shard_map/all_to_all | solution.py:22
  57.2 26.9 %collective-permute-start.3 = (bf16[4,128,256]{2,1,0:T(8,128)(2,1)}, bf16[4,128,256]{2,1,0:T(8,128)(2,1)S(1)}, u32[]{:S(2)}, u32[]{:S(2)}) collective-permute-start(bf16[4,128,256]{2,1,0:T(8,128)(2,1)} %get-tuple-element.40), channel_id=1, source_target_pairs={{0,64},{32,96},{64,0},{96,32},{1,65},{33,97},{65,1},{97,33},{2,66}... | collective-permute-start | bytes 786440 | tf_op jit(solution)/shard_map/ppermute | solution.py:202
  60.8 25.9 %collective-permute-start.4 = (bf16[4,128,256]{2,1,0:T(8,128)(2,1)}, bf16[4,128,256]{2,1,0:T(8,128)(2,1)S(1)}, u32[]{:S(2)}, u32[]{:S(2)}) collective-permute-start(bf16[4,128,256]{2,1,0:T(8,128)(2,1)} %get-tuple-element.41), channel_id=1, source_target_pairs={{0,32},{32,64},{64,96},{96,0},{1,33},{33,65},{65,97},{97,1},{2,34}... | collective-permute-start | bytes 786440 | tf_op jit(solution)/shard_map/ppermute | solution.py:202
  61.5 25.2 %collective-permute-start.5 = (bf16[4,128,256]{2,1,0:T(8,128)(2,1)}, bf16[4,128,256]{2,1,0:T(8,128)(2,1)S(1)}, u32[]{:S(2)}, u32[]{:S(2)}) collective-permute-start(bf16[4,128,256]{2,1,0:T(8,128)(2,1)} %get-tuple-element.42), channel_id=1, source_target_pairs={{0,96},{32,0},{64,32},{96,64},{1,97},{33,1},{65,33},{97,65},{2,98}... | collective-permute-start | bytes 786440 | tf_op jit(solution)/shard_map/ppermute | solution.py:202
  79.9 10.6 %collective-permute-start = (bf16[4,128,256]{2,1,0:T(8,128)(2,1)}, bf16[4,128,256]{2,1,0:T(8,128)(2,1)S(1)}, u32[]{:S(2)}, u32[]{:S(2)}) collective-permute-start(bf16[4,128,256]{2,1,0:T(8,128)(2,1)} %get-tuple-element.36), channel_id=1, source_target_pairs={{0,64},{32,96},{64,0},{96,32},{1,65},{33,97},{65,1},{97,33},{2,66}... | collective-permute-start | bytes 786440 | tf_op jit(solution)/shard_map/ppermute | solution.py:202
  83.4 13.1 %collective-permute-start.1 = (bf16[4,128,256]{2,1,0:T(8,128)(2,1)}, bf16[4,128,256]{2,1,0:T(8,128)(2,1)S(1)}, u32[]{:S(2)}, u32[]{:S(2)}) collective-permute-start(bf16[4,128,256]{2,1,0:T(8,128)(2,1)} %get-tuple-element.37), channel_id=1, source_target_pairs={{0,32},{32,64},{64,96},{96,0},{1,33},{33,65},{65,97},{97,1},{2,34}... | collective-permute-start | bytes 786440 | tf_op jit(solution)/shard_map/ppermute | solution.py:202
  84.1 12.5 %collective-permute-start.2 = (bf16[4,128,256]{2,1,0:T(8,128)(2,1)}, bf16[4,128,256]{2,1,0:T(8,128)(2,1)S(1)}, u32[]{:S(2)}, u32[]{:S(2)}) collective-permute-start(bf16[4,128,256]{2,1,0:T(8,128)(2,1)} %get-tuple-element.38), channel_id=1, source_target_pairs={{0,96},{32,0},{64,32},{96,64},{1,97},{33,1},{65,33},{97,65},{2,98}... | collective-permute-start | bytes 786440 | tf_op jit(solution)/shard_map/ppermute | solution.py:202
  105.6 32.7 %all-to-all-start.3 = ((bf16[32,128,256]{2,1,0:T(8,128)(2,1)}), bf16[32,128,256]{2,1,0:T(8,128)(2,1)}, u32[]{:S(2)}, u32[]{:S(2)}) async-start(bf16[32,128,256]{2,1,0:T(8,128)(2,1)} %pick.7), calls=%async_computation.3 | async-start | bytes 4194304 | tf_op jit(solution)/shard_map/all_to_all | solution.py:22
  138.3 35.1 %all-to-all-start.2 = ((bf16[32,128,256]{2,1,0:T(8,128)(2,1)}), bf16[32,128,256]{2,1,0:T(8,128)(2,1)}, u32[]{:S(2)}, u32[]{:S(2)}) async-start(bf16[32,128,256]{2,1,0:T(8,128)(2,1)} %pick.6), calls=%async_computation.2 | async-start | bytes 4194304 | tf_op jit(solution)/shard_map/all_to_all | solution.py:22
  152.6 30.5 %collective-permute-start.9 = (bf16[4,128,256]{2,1,0:T(8,128)(2,1)}, bf16[4,128,256]{2,1,0:T(8,128)(2,1)S(1)}, u32[]{:S(2)}, u32[]{:S(2)}) collective-permute-start(bf16[4,128,256]{2,1,0:T(8,128)(2,1)} %get-tuple-element.48), channel_id=1, source_target_pairs={{0,64},{32,96},{64,0},{96,32},{1,65},{33,97},{65,1},{97,33},{2,66}... | collective-permute-start | bytes 786440 | tf_op jit(solution)/shard_map/ppermute | solution.py:202
  155.0 29.9 %collective-permute-start.10 = (bf16[4,128,256]{2,1,0:T(8,128)(2,1)}, bf16[4,128,256]{2,1,0:T(8,128)(2,1)S(1)}, u32[]{:S(2)}, u32[]{:S(2)}) collective-permute-start(bf16[4,128,256]{2,1,0:T(8,128)(2,1)} %get-tuple-element.49), channel_id=1, source_target_pairs={{0,32},{32,64},{64,96},{96,0},{1,33},{33,65},{65,97},{97,1},{2,34}... | collective-permute-start | bytes 786440 | tf_op jit(solution)/shard_map/ppermute | solution.py:202
  156.5 28.5 %collective-permute-start.11 = (bf16[4,128,256]{2,1,0:T(8,128)(2,1)}, bf16[4,128,256]{2,1,0:T(8,128)(2,1)S(1)}, u32[]{:S(2)}, u32[]{:S(2)}) collective-permute-start(bf16[4,128,256]{2,1,0:T(8,128)(2,1)} %get-tuple-element.50), channel_id=1, source_target_pairs={{0,96},{32,0},{64,32},{96,64},{1,97},{33,1},{65,33},{97,65},{2,98}... | collective-permute-start | bytes 786440 | tf_op jit(solution)/shard_map/ppermute | solution.py:202
  179.3 9.6 %collective-permute-start.6 = (bf16[4,128,256]{2,1,0:T(8,128)(2,1)}, bf16[4,128,256]{2,1,0:T(8,128)(2,1)S(1)}, u32[]{:S(2)}, u32[]{:S(2)}) collective-permute-start(bf16[4,128,256]{2,1,0:T(8,128)(2,1)} %get-tuple-element.44), channel_id=1, source_target_pairs={{0,64},{32,96},{64,0},{96,32},{1,65},{33,97},{65,1},{97,33},{2,66}... | collective-permute-start | bytes 786440 | tf_op jit(solution)/shard_map/ppermute | solution.py:202
  181.7 14.2 %collective-permute-start.7 = (bf16[4,128,256]{2,1,0:T(8,128)(2,1)}, bf16[4,128,256]{2,1,0:T(8,128)(2,1)S(1)}, u32[]{:S(2)}, u32[]{:S(2)}) collective-permute-start(bf16[4,128,256]{2,1,0:T(8,128)(2,1)} %get-tuple-element.45), channel_id=1, source_target_pairs={{0,32},{32,64},{64,96},{96,0},{1,33},{33,65},{65,97},{97,1},{2,34}... | collective-permute-start | bytes 786440 | tf_op jit(solution)/shard_map/ppermute | solution.py:202
  183.2 12.8 %collective-permute-start.8 = (bf16[4,128,256]{2,1,0:T(8,128)(2,1)}, bf16[4,128,256]{2,1,0:T(8,128)(2,1)S(1)}, u32[]{:S(2)}, u32[]{:S(2)}) collective-permute-start(bf16[4,128,256]{2,1,0:T(8,128)(2,1)} %get-tuple-element.46), channel_id=1, source_target_pairs={{0,96},{32,0},{64,32},{96,64},{1,97},{33,1},{65,33},{97,65},{2,98}... | collective-permute-start | bytes 786440 | tf_op jit(solution)/shard_map/ppermute | solution.py:202
  204.0 41.8 %copy-start.11 = (bf16[4,128,256]{2,1,0:T(8,128)(2,1)}, bf16[4,128,256]{2,1,0:T(8,128)(2,1)S(1)}, u32[]{:S(2)}) copy-start(bf16[4,128,256]{2,1,0:T(8,128)(2,1)S(1)} %get-tuple-element.52.refs_0_) | copy-start | bytes 786436
  204.1 9.9 %collective-permute-start.14 = (bf16[4,128,256]{2,1,0:T(8,128)(2,1)S(1)}, bf16[4,128,256]{2,1,0:T(8,128)(2,1)S(1)}, u32[]{:S(2)}, u32[]{:S(2)}) collective-permute-start(bf16[4,128,256]{2,1,0:T(8,128)(2,1)S(1)} %get-tuple-element.106.refs_0_), channel_id=1, source_target_pairs={{0,32},{32,64},{64,96},{96,0},{1,33},{33,65},{65,97},{97,1},{2,34}... | collective-permute-start | bytes 786440 | tf_op jit(solution)/shard_map/ppermute | solution.py:202
  205.1 14.7 %collective-permute-start.13 = (bf16[4,128,256]{2,1,0:T(8,128)(2,1)S(1)}, bf16[4,128,256]{2,1,0:T(8,128)(2,1)}, u32[]{:S(2)}, u32[]{:S(2)}) collective-permute-start(bf16[4,128,256]{2,1,0:T(8,128)(2,1)S(1)} %get-tuple-element.106.refs_0_), channel_id=1, source_target_pairs={{0,64},{32,96},{64,0},{96,32},{1,65},{33,97},{65,1},{97,33},{2,66}... | collective-permute-start | bytes 786440 | tf_op jit(solution)/shard_map/ppermute | solution.py:202
  207.9 12.0 %collective-permute-start.12 = (bf16[4,128,256]{2,1,0:T(8,128)(2,1)S(1)}, bf16[4,128,256]{2,1,0:T(8,128)(2,1)}, u32[]{:S(2)}, u32[]{:S(2)}) collective-permute-start(bf16[4,128,256]{2,1,0:T(8,128)(2,1)S(1)} %get-tuple-element.106.refs_0_), channel_id=1, source_target_pairs={{0,96},{32,0},{64,32},{96,64},{1,97},{33,1},{65,33},{97,65},{2,98}... | collective-permute-start | bytes 786440 | tf_op jit(solution)/shard_map/ppermute | solution.py:202
  226.6 41.3 %all-to-all-start.4 = ((bf16[32,128,256]{2,1,0:T(8,128)(2,1)}), bf16[32,128,256]{2,1,0:T(8,128)(2,1)}, u32[]{:S(2)}, u32[]{:S(2)}) async-start(bf16[32,128,256]{2,1,0:T(8,128)(2,1)} %tiles_t.4), calls=%async_computation.4 | async-start | bytes 4194304 | tf_op jit(solution)/shard_map/all_to_all | solution.py:22
  243.6 15.1 %collective-permute-start.17 = (bf16[4,128,256]{2,1,0:T(8,128)(2,1)S(1)}, bf16[4,128,256]{2,1,0:T(8,128)(2,1)S(1)}, u32[]{:S(2)}, u32[]{:S(2)}) collective-permute-start(bf16[4,128,256]{2,1,0:T(8,128)(2,1)S(1)} %get-tuple-element.52.refs_0_), channel_id=1, source_target_pairs={{0,32},{32,64},{64,96},{96,0},{1,33},{33,65},{65,97},{97,1},{2,34}... | collective-permute-start | bytes 786440 | tf_op jit(solution)/shard_map/ppermute | solution.py:202
  243.6 15.2 %collective-permute-start.16 = (bf16[4,128,256]{2,1,0:T(8,128)(2,1)S(1)}, bf16[4,128,256]{2,1,0:T(8,128)(2,1)S(1)}, u32[]{:S(2)}, u32[]{:S(2)}) collective-permute-start(bf16[4,128,256]{2,1,0:T(8,128)(2,1)S(1)} %get-tuple-element.52.refs_0_), channel_id=1, source_target_pairs={{0,64},{32,96},{64,0},{96,32},{1,65},{33,97},{65,1},{97,33},{2,66}... | collective-permute-start | bytes 786440 | tf_op jit(solution)/shard_map/ppermute | solution.py:202
  245.8 14.3 %collective-permute-start.15 = (bf16[4,128,256]{2,1,0:T(8,128)(2,1)S(1)}, bf16[4,128,256]{2,1,0:T(8,128)(2,1)}, u32[]{:S(2)}, u32[]{:S(2)}) collective-permute-start(bf16[4,128,256]{2,1,0:T(8,128)(2,1)S(1)} %get-tuple-element.52.refs_0_), channel_id=1, source_target_pairs={{0,96},{32,0},{64,32},{96,64},{1,97},{33,1},{65,33},{97,65},{2,98}... | collective-permute-start | bytes 786440 | tf_op jit(solution)/shard_map/ppermute | solution.py:202
  266.9 9.1 %collective-permute-start.18 = (bf16[256,2048]{1,0:T(8,128)(2,1)S(1)}, bf16[256,2048]{1,0:T(8,128)(2,1)}, u32[]{:S(2)}, u32[]{:S(2)}) collective-permute-start(bf16[256,2048]{1,0:T(8,128)(2,1)S(1)} %copy-done.9), channel_id=1, source_target_pairs={{0,1},{1,0},{2,3},{3,2},{4,5},{5,4},{6,7},{7,6},{8,9},{9,8},{10,11... | collective-permute-start | bytes 3145736 | tf_op jit(solution)/shard_map/ppermute | solution.py:202
  267.9 34.3 %all-to-all-start.5 = ((bf16[32,128,256]{2,1,0:T(8,128)(2,1)}), bf16[32,128,256]{2,1,0:T(8,128)(2,1)}, u32[]{:S(2)}, u32[]{:S(2)}) async-start(bf16[32,128,256]{2,1,0:T(8,128)(2,1)} %tiles_t.5), calls=%async_computation.5 | async-start | bytes 4194304 | tf_op jit(solution)/shard_map/all_to_all | solution.py:22
  279.0 15.2 %collective-permute-start.19 = (bf16[64,2048]{1,0:T(8,128)(2,1)S(1)}, bf16[64,2048]{1,0:T(8,128)(2,1)S(1)}, u32[]{:S(2)}, u32[]{:S(2)}) collective-permute-start(bf16[64,2048]{1,0:T(8,128)(2,1)S(1)} %get-tuple-element.86), channel_id=1, source_target_pairs={{0,32},{32,64},{64,96},{96,0},{1,33},{33,65},{65,97},{97,1},{2,34}... | collective-permute-start | bytes 786440 | tf_op jit(solution)/shard_map/ppermute | solution.py:202
  279.1 15.1 %collective-permute-start.21 = (bf16[64,2048]{1,0:T(8,128)(2,1)S(1)}, bf16[64,2048]{1,0:T(8,128)(2,1)S(1)}, u32[]{:S(2)}, u32[]{:S(2)}) collective-permute-start(bf16[64,2048]{1,0:T(8,128)(2,1)S(1)} %get-tuple-element.87), channel_id=1, source_target_pairs={{0,96},{32,0},{64,32},{96,64},{1,97},{33,1},{65,33},{97,65},{2,98}... | collective-permute-start | bytes 786440 | tf_op jit(solution)/shard_map/ppermute | solution.py:202
  282.3 11.9 %collective-permute-start.20 = (bf16[64,2048]{1,0:T(8,128)(2,1)S(1)}, bf16[64,2048]{1,0:T(8,128)(2,1)}, u32[]{:S(2)}, u32[]{:S(2)}) collective-permute-start(bf16[64,2048]{1,0:T(8,128)(2,1)S(1)} %get-tuple-element.88), channel_id=1, source_target_pairs={{0,64},{32,96},{64,0},{96,32},{1,65},{33,97},{65,1},{97,33},{2,66}... | collective-permute-start | bytes 786440 | tf_op jit(solution)/shard_map/ppermute | solution.py:202
  312.5 52.2 %copy-start.10 = (bf16[4,128,256]{2,1,0:T(8,128)(2,1)}, bf16[4,128,256]{2,1,0:T(8,128)(2,1)S(1)}, u32[]{:S(2)}) copy-start(bf16[4,128,256]{2,1,0:T(8,128)(2,1)S(1)} %get-tuple-element.60.refs_0_) | copy-start | bytes 786436
  312.5 16.3 %collective-permute-start.24 = (bf16[4,128,256]{2,1,0:T(8,128)(2,1)}, bf16[4,128,256]{2,1,0:T(8,128)(2,1)}, u32[]{:S(2)}, u32[]{:S(2)}) collective-permute-start(bf16[4,128,256]{2,1,0:T(8,128)(2,1)} %get-tuple-element.104.refs_0_), channel_id=1, source_target_pairs={{0,32},{32,64},{64,96},{96,0},{1,33},{33,65},{65,97},{97,1},{2,34}... | collective-permute-start | bytes 786440 | tf_op jit(solution)/shard_map/ppermute | solution.py:202
  312.5 16.3 %collective-permute-start.23 = (bf16[4,128,256]{2,1,0:T(8,128)(2,1)}, bf16[4,128,256]{2,1,0:T(8,128)(2,1)}, u32[]{:S(2)}, u32[]{:S(2)}) collective-permute-start(bf16[4,128,256]{2,1,0:T(8,128)(2,1)} %get-tuple-element.104.refs_0_), channel_id=1, source_target_pairs={{0,64},{32,96},{64,0},{96,32},{1,65},{33,97},{65,1},{97,33},{2,66}... | collective-permute-start | bytes 786440 | tf_op jit(solution)/shard_map/ppermute | solution.py:202
  314.2 15.2 %collective-permute-start.22 = (bf16[4,128,256]{2,1,0:T(8,128)(2,1)}, bf16[4,128,256]{2,1,0:T(8,128)(2,1)}, u32[]{:S(2)}, u32[]{:S(2)}) collective-permute-start(bf16[4,128,256]{2,1,0:T(8,128)(2,1)} %get-tuple-element.104.refs_0_), channel_id=1, source_target_pairs={{0,96},{32,0},{64,32},{96,64},{1,97},{33,1},{65,33},{97,65},{2,98}... | collective-permute-start | bytes 786440 | tf_op jit(solution)/shard_map/ppermute | solution.py:202
  336.1 8.4 %collective-permute-start.28 = (bf16[256,2048]{1,0:T(8,128)(2,1)}, bf16[256,2048]{1,0:T(8,128)(2,1)}, u32[]{:S(2)}, u32[]{:S(2)}) collective-permute-start(bf16[256,2048]{1,0:T(8,128)(2,1)} %pad_maximum_fusion.1), channel_id=1, source_target_pairs={{0,1},{1,0},{2,3},{3,2},{4,5},{5,4},{6,7},{7,6},{8,9},{9,8},{10,11... | collective-permute-start | bytes 3145736 | tf_op jit(solution)/shard_map/ppermute | solution.py:202
  337.6 46.2 %all-to-all-start.6 = ((bf16[32,128,256]{2,1,0:T(8,128)(2,1)}), bf16[32,128,256]{2,1,0:T(8,128)(2,1)S(1)}, u32[]{:S(2)}, u32[]{:S(2)}) async-start(bf16[32,128,256]{2,1,0:T(8,128)(2,1)} %tiles_t.6), calls=%async_computation.6 | async-start | bytes 4194304 | tf_op jit(solution)/shard_map/all_to_all | solution.py:22
  348.3 16.3 %collective-permute-start.29 = (bf16[64,2048]{1,0:T(8,128)(2,1)}, bf16[64,2048]{1,0:T(8,128)(2,1)}, u32[]{:S(2)}, u32[]{:S(2)}) collective-permute-start(bf16[64,2048]{1,0:T(8,128)(2,1)} %get-tuple-element.83), channel_id=1, source_target_pairs={{0,32},{32,64},{64,96},{96,0},{1,33},{33,65},{65,97},{97,1},{2,34}... | collective-permute-start | bytes 786440 | tf_op jit(solution)/shard_map/ppermute | solution.py:202
  348.3 21.2 %collective-permute-start.31 = (bf16[64,2048]{1,0:T(8,128)(2,1)S(1)}, bf16[64,2048]{1,0:T(8,128)(2,1)}, u32[]{:S(2)}, u32[]{:S(2)}) collective-permute-start(bf16[64,2048]{1,0:T(8,128)(2,1)S(1)} %get-tuple-element.84), channel_id=1, source_target_pairs={{0,96},{32,0},{64,32},{96,64},{1,97},{33,1},{65,33},{97,65},{2,98}... | collective-permute-start | bytes 786440 | tf_op jit(solution)/shard_map/ppermute | solution.py:202
  351.5 17.9 %collective-permute-start.30 = (bf16[64,2048]{1,0:T(8,128)(2,1)S(1)}, bf16[64,2048]{1,0:T(8,128)(2,1)}, u32[]{:S(2)}, u32[]{:S(2)}) collective-permute-start(bf16[64,2048]{1,0:T(8,128)(2,1)S(1)} %get-tuple-element.85), channel_id=1, source_target_pairs={{0,64},{32,96},{64,0},{96,32},{1,65},{33,97},{65,1},{97,33},{2,66}... | collective-permute-start | bytes 786440 | tf_op jit(solution)/shard_map/ppermute | solution.py:202
  351.5 23.4 %collective-permute-start.27 = (bf16[4,128,256]{2,1,0:T(8,128)(2,1)S(1)}, bf16[4,128,256]{2,1,0:T(8,128)(2,1)S(1)}, u32[]{:S(2)}, u32[]{:S(2)}) collective-permute-start(bf16[4,128,256]{2,1,0:T(8,128)(2,1)S(1)} %get-tuple-element.60.refs_0_), channel_id=1, source_target_pairs={{0,32},{32,64},{64,96},{96,0},{1,33},{33,65},{65,97},{97,1},{2,34}... | collective-permute-start | bytes 786440 | tf_op jit(solution)/shard_map/ppermute | solution.py:202
  352.6 24.5 %collective-permute-start.26 = (bf16[4,128,256]{2,1,0:T(8,128)(2,1)S(1)}, bf16[4,128,256]{2,1,0:T(8,128)(2,1)}, u32[]{:S(2)}, u32[]{:S(2)}) collective-permute-start(bf16[4,128,256]{2,1,0:T(8,128)(2,1)S(1)} %get-tuple-element.60.refs_0_), channel_id=1, source_target_pairs={{0,64},{32,96},{64,0},{96,32},{1,65},{33,97},{65,1},{97,33},{2,66}... | collective-permute-start | bytes 786440 | tf_op jit(solution)/shard_map/ppermute | solution.py:202
  364.6 12.5 %collective-permute-start.25 = (bf16[4,128,256]{2,1,0:T(8,128)(2,1)S(1)}, bf16[4,128,256]{2,1,0:T(8,128)(2,1)}, u32[]{:S(2)}, u32[]{:S(2)}) collective-permute-start(bf16[4,128,256]{2,1,0:T(8,128)(2,1)S(1)} %get-tuple-element.60.refs_0_), channel_id=1, source_target_pairs={{0,96},{32,0},{64,32},{96,64},{1,97},{33,1},{65,33},{97,65},{2,98}... | collective-permute-start | bytes 786440 | tf_op jit(solution)/shard_map/ppermute | solution.py:202
  371.6 21.6 %collective-permute-start.32 = (bf16[16,4096]{1,0:T(8,128)(2,1)}, bf16[16,4096]{1,0:T(8,128)(2,1)}, u32[]{:S(2)}, u32[]{:S(2)}) collective-permute-start(bf16[16,4096]{1,0:T(8,128)(2,1)} %get-tuple-element.89), channel_id=1, source_target_pairs={{0,8},{8,16},{16,24},{24,0},{1,9},{9,17},{17,25},{25,1},{2,10},{10... | collective-permute-start | bytes 393224 | tf_op jit(solution)/shard_map/ppermute | solution.py:202
  373.1 20.2 %collective-permute-start.33 = (bf16[16,4096]{1,0:T(8,128)(2,1)}, bf16[16,4096]{1,0:T(8,128)(2,1)}, u32[]{:S(2)}, u32[]{:S(2)}) collective-permute-start(bf16[16,4096]{1,0:T(8,128)(2,1)} %get-tuple-element.90), channel_id=1, source_target_pairs={{0,16},{8,24},{16,0},{24,8},{1,17},{9,25},{17,1},{25,9},{2,18},{10... | collective-permute-start | bytes 393224 | tf_op jit(solution)/shard_map/ppermute | solution.py:202
  375.6 17.7 %collective-permute-start.34 = (bf16[16,4096]{1,0:T(8,128)(2,1)S(1)}, bf16[16,4096]{1,0:T(8,128)(2,1)}, u32[]{:S(2)}, u32[]{:S(2)}) collective-permute-start(bf16[16,4096]{1,0:T(8,128)(2,1)S(1)} %get-tuple-element.91), channel_id=1, source_target_pairs={{0,24},{8,0},{16,8},{24,16},{1,25},{9,1},{17,9},{25,17},{2,26},{10... | collective-permute-start | bytes 393224 | tf_op jit(solution)/shard_map/ppermute | solution.py:202
  385.1 42.3 %all-to-all-start.7 = ((bf16[32,128,256]{2,1,0:T(8,128)(2,1)}), bf16[32,128,256]{2,1,0:T(8,128)(2,1)}, u32[]{:S(2)}, u32[]{:S(2)}) async-start(bf16[32,128,256]{2,1,0:T(8,128)(2,1)} %tiles_t.7), calls=%async_computation.7 | async-start | bytes 4194304 | tf_op jit(solution)/shard_map/all_to_all | solution.py:22
  394.5 24.3 %collective-permute-start.35 = (bf16[4,4096]{1,0:T(4,128)(2,1)S(1)}, bf16[4,4096]{1,0:T(4,128)(2,1)S(1)}, u32[]{:S(2)}, u32[]{:S(2)}) collective-permute-start(bf16[4,4096]{1,0:T(4,128)(2,1)S(1)} %get-tuple-element.108), channel_id=1, source_target_pairs={{0,2},{2,4},{4,6},{6,0},{1,3},{3,5},{5,7},{7,1},{8,10},{10,12},{12... | collective-permute-start | bytes 98312 | tf_op jit(solution)/shard_map/ppermute | solution.py:202
  396.0 24.5 %collective-permute-start.37 = (bf16[4,4096]{1,0:T(4,128)(2,1)S(1)}, bf16[4,4096]{1,0:T(4,128)(2,1)S(1)}, u32[]{:S(2)}, u32[]{:S(2)}) collective-permute-start(bf16[4,4096]{1,0:T(4,128)(2,1)S(1)} %get-tuple-element.109), channel_id=1, source_target_pairs={{0,6},{2,0},{4,2},{6,4},{1,7},{3,1},{5,3},{7,5},{8,14},{10,8},{12,... | collective-permute-start | bytes 98312 | tf_op jit(solution)/shard_map/ppermute | solution.py:202
  397.8 25.2 %collective-permute-start.36 = (bf16[4,4096]{1,0:T(4,128)(2,1)S(1)}, bf16[4,4096]{1,0:T(4,128)(2,1)S(1)}, u32[]{:S(2)}, u32[]{:S(2)}) collective-permute-start(bf16[4,4096]{1,0:T(4,128)(2,1)S(1)} %get-tuple-element.110), channel_id=1, source_target_pairs={{0,4},{2,6},{4,0},{6,2},{1,5},{3,7},{5,1},{7,3},{8,12},{10,14},{12... | collective-permute-start | bytes 98312 | tf_op jit(solution)/shard_map/ppermute | solution.py:202
  (31 other events, 229.7 us)
